TPU v7x, 32 devices: a whole 2x2x4 slice. The times are simulated.
32 devices in a mesh: dp: 4 (over y, x), tp: 8 (over z, core).
Axes of the slice: x: 2, y: 2, z: 4, core: 2. Of those that a mesh axis runs over, the one named last changes fastest.
Arguments:
- gate_pre: bfloat16 [1024, 28672], P('dp', 'tp'), may hold values from -9 to 9
- up_pre: bfloat16 [1024, 28672], P('dp', 'tp'), may hold values from -9 to 9
- token_live: int32 [1024], P('dp'), may hold values from 0 to 1, as said below
- slab_offset: int32 [8], replicated, may hold values from 0 to 2048
Outputs:
- slab_cov: float32 [28672, 12288], P('dp', 'tp')
Inputs may be any that keep to these rules, and one draw needn't show every extreme that they name: `token_live`: the first token of each block of 256 tokens is live.
All inputs are finite; a program needn't handle non-finite values.
Results may differ from a plain program's by a relative error of at most 0.004.
Values may be sent and summed in bfloat16 or wider, within the bound.
No kernel may reach another device: no remote copies, remote signals or barrier semaphores. Data moves between devices by JAX's collectives and lax.ppermute only.
A program may use at most 192 MiB of HBM per device.

v0:
```python
import jax
import jax.numpy as jnp
from jax import lax
from jax.sharding import PartitionSpec as P

SLAB_DEV = 1536


def contract_tokens(left, right):
    return lax.dot_general(
        left, right, (((0,), (0,)), ((), ())), preferred_element_type=jnp.float32
    )


def on_device(gate_pre, up_pre, token_live, slab_offset):
    live_mask = token_live.astype(jnp.float32)
    key_local = (
        jax.nn.silu(gate_pre.astype(jnp.float32)) * up_pre.astype(jnp.float32) * live_mask[:, None]
    ).astype(jnp.bfloat16)
    live_total = lax.psum(jnp.sum(live_mask), "dp")
    offset_here = slab_offset[lax.axis_index("tp")]
    slab_keys = lax.dynamic_slice_in_dim(key_local, offset_here, SLAB_DEV, 1)
    all_keys = lax.all_gather(key_local, "tp", axis=1, tiled=True)
    key_block = lax.all_to_all(all_keys, "dp", split_axis=1, concat_axis=0, tiled=True)
    slab_all = lax.all_gather(slab_keys, "dp", axis=0, tiled=True)
    gram_slab = contract_tokens(key_block, slab_all)
    return gram_slab / live_total


def solution(mesh):
    placed = (P("dp", "tp"), P("dp", "tp"), P("dp"), P())
    return jax.shard_map(
        on_device, mesh=mesh, in_specs=placed, out_specs=P("dp", "tp"), check_vma=False
    )
```

profile of v0, /device:TPU:0, one launch (start us, length us, event | category | flops | bytes accessed | tf_op | source)
XLA Modules:
  0.0 410.6 jit_solution(5511081595611352815)
XLA Ops:
  7.4 0.0 all-gather.3.cloned.1.call-start
  7.4 0.7 convert_element_type.14
  8.1 2.9 copy.5
  10.9 3.8 copy.6
  14.7 3.9 fusion.5
  18.7 0.0 all-gather.3.cloned.1.call-update
  18.7 136.8 %all-gather.3.cloned.1.call-done = bf16[256,28672]{0,1:T(8,128)(2,1)} async-done(((bf16[256,3584]{0,1:T(8,128)(2,1)}), bf16[256,28672]{0,1:T(8,128)(2,1)}) %all-gather.3.cloned.1.call-update) | async-done | bytes 14680080 | tf_op jit(solution)/shard_map/all_gather | solution.py:23
  155.5 0.0 copy-start.1
  155.5 0.0 copy-start
  155.5 6.8 %all-to-all-start = ((bf16[256,4,7168]{0,2,1:T(8,128)(2,1)}), bf16[256,4,7168]{0,2,1:T(8,128)(2,1)}, u32[]{:S(2)}, u32[]{:S(2)}) async-start(bf16[256,4,7168]{0,2,1:T(8,128)(2,1)} %bitcast.6), calls=%async_computation | async-start | bytes 29360128 | tf_op jit(solution)/shard_map/all_to_all | solution.py:24
  162.3 0.0 all-gather.5.cloned.1.call-start
  162.3 0.0 copy-done.1
  162.3 0.6 dynamic_slice.6
  164.8 2.2 constant_dynamic-slice_fusion
  167.1 0.0 all-gather.5.cloned.1.call-update
  167.1 0.0 copy-done
  167.1 0.6 convert_reduce_fusion
  167.7 183.9 %psum.7 = f32[]{:T(128)} all-reduce(f32[]{:T(128)} %convert_reduce_fusion), channel_id=1, replica_groups=mesh['dp'=4,'tp'=8] {'dp'}, use_global_device_ids=true, to_apply=%region_1.2 | all-reduce | flops 1 | bytes 8 | tf_op jit(solution)/shard_map/psum | solution.py:20
  351.6 0.0 all-to-all-done
  351.6 19.7 %copy.7 = bf16[4,256,7168]{2,1,0:T(8,128)(2,1)} copy(bf16[4,256,7168]{1,2,0:T(8,128)(2,1)} %bitcast.1) | data formatting | bytes 29360128 | tf_op jit(solution)/shard_map/all_to_all | solution.py:24
  371.4 0.0 all-gather.5.cloned.1.call-done
  371.4 31.8 %convolution_divide_fusion = f32[7168,1536]{1,0:T(8,128)} fusion(bf16[1024,7168]{1,0:T(8,128)(2,1)} %bitcast.7, bf16[1024,1536]{0,1:T(8,128)(2,1)} %all-gather.5.cloned.1.call-done, f32[]{:T(128)} %psum.7), kind=kOutput, calls=%fused_computation | convolution fusion | flops 22559588352 | bytes 61865988 | tf_op jit(solution)/shard_map/dot_general | solution.py:10
Async XLA Ops:
  7.4 148.1 %all-gather.3.cloned.1.call-start = ((), (), s32[]{:S(2)}) async-start(), calls=%async_computation.1 | async-start | bytes 16515072 | tf_op jit(solution)/shard_map/all_gather | solution.py:23
  155.5 6.8 %copy-start.1 = (s32[8]{0:T(128)S(1)}, s32[8]{0:T(128)}, u32[]{:S(2)}) copy-start(s32[8]{0:T(128)} %param.7) | copy-start | bytes 100
  155.5 11.6 %copy-start = (s32[256]{0:T(256)S(1)}, s32[256]{0:T(256)}, u32[]{:S(2)}) copy-start(s32[256]{0:T(256)} %param.6) | copy-start | bytes 3076
  155.5 196.1 %all-to-all-start = ((bf16[256,4,7168]{0,2,1:T(8,128)(2,1)}), bf16[256,4,7168]{0,2,1:T(8,128)(2,1)}, u32[]{:S(2)}, u32[]{:S(2)}) async-start(bf16[256,4,7168]{0,2,1:T(8,128)(2,1)} %bitcast.6), calls=%async_computation | async-start | bytes 29360128 | tf_op jit(solution)/shard_map/all_to_all | solution.py:24
  162.3 209.1 %all-gather.5.cloned.1.call-start = ((), (), s32[]{:S(2)}) async-start(), calls=%async_computation.2 | async-start | bytes 3932160 | tf_op jit(solution)/shard_map/all_gather | solution.py:25
Sparse Core Ops, SparseCore 0:
  18.8 136.6 all-gather.2
Sparse Core Ops, SparseCore 1:
  167.2 132.7 all-gather.4
where the time goes:
time: 412 us; the launch traced here: 411 us
  blocking collectives  184 us (45%)
  waiting for transfers between devices  137 us (33%)
  matrix products  31.8 us (8%)
  local copies, waits for them, and re-layouts  29.3 us (7%)
  between operations  16.7 us (4%)
  starting transfers between devices  6.82 us (2%)
  other arithmetic  5.23 us (1%)
    psum x1, blocking collectives, on_device(): live_total = lax.psum(jnp.sum(live_mask), 'dp')  184 us
    all_gather x1, waiting for transfers between devices, on_device(): all_keys = lax.all_gather(key_local, 'tp', axis=1, tiled=True)  137 us
    dot_general x1, matrix products, contract_tokens(): lax.dot_general(left, right, (((0,), (0,)), ((), ())), preferred_element_...  31.8 us
    all_to_all x1, local copies, waits for them, and re-layouts, on_device(): lax.all_to_all(all_keys, 'dp', split_axis=1, concat_axis=0, tiled=True)  19.7 us
  transfers between devices with their start and end apart: 3, of which 1 were waited for; matrix products, arithmetic and copies ran while one was open for 6% of the time, Pallas kernels for 0%

commit v1 on v0

v1 whole, which is shorter than its diff:
```python
import functools

import jax
import jax.numpy as jnp
from jax import lax
from jax.experimental import pallas as pl
from jax.experimental.pallas import tpu as pltpu
from jax.sharding import PartitionSpec as P

SLAB_DEV = 1536
UNIT = 256
SLOTS = 4


def keys_kernel(room, cuts, live_ref, gate_ref, up_ref, *refs):
    own_refs, spare_refs, order_ref = refs[: len(cuts) - 1], refs[len(cuts) - 1 : -1], refs[-1]
    tokens = gate_ref.shape[0]
    step = pl.program_id(0)

    @pl.when(step == 0)
    def _():
        live = live_ref[...].astype(jnp.float32)
        slot_id = lax.broadcasted_iota(jnp.int32, (tokens, tokens), 0)
        token_id = lax.broadcasted_iota(jnp.int32, (tokens, tokens), 1)
        upto = (slot_id <= token_id).astype(jnp.float32)
        rank = (jnp.dot(jnp.broadcast_to(live, (8, tokens)), upto, preferred_element_type=jnp.float32) - 1.0)[:1]
        total = jnp.sum(live)
        slot = jnp.where(rank < room, rank, tokens - total + rank)
        taken = (slot_id.astype(jnp.float32) == slot) & (live > 0)
        order_ref[...] = taken.astype(jnp.bfloat16)

    gate = gate_ref[...].astype(jnp.float32)
    key = gate / (1.0 + jnp.exp(-gate)) * up_ref[...].astype(jnp.float32)
    placed = jnp.dot(
        order_ref[...], key.astype(jnp.bfloat16), preferred_element_type=jnp.float32
    ).astype(jnp.bfloat16)
    for c in range(len(cuts) - 1):

        @pl.when((step >= cuts[c]) & (step < cuts[c + 1]))
        def _(c=c):
            own_refs[c][...] = placed[:room]

    @pl.when(step < cuts[1])
    def _():
        spare_refs[0][...] = placed[room:]

    @pl.when(step >= cuts[1])
    def _():
        spare_refs[1][...] = placed[room:]


def live_keys(gate_pre, up_pre, token_live, room, widths):
    tokens, width = gate_pre.shape
    spare = tokens - room
    cuts = [sum(widths[:i]) // UNIT for i in range(len(widths) + 1)]
    spans = [(cuts[i], cuts[i + 1]) for i in range(len(widths))]
    spare_spans = [(0, cuts[1]), (cuts[1], cuts[-1])]

    def spec(height, span):
        low, high = span
        return pl.BlockSpec((height, UNIT), lambda i: (0, jnp.clip(i - low, 0, high - low - 1)))

    def shape(height, span):
        return jax.ShapeDtypeStruct((height, (span[1] - span[0]) * UNIT), jnp.bfloat16)

    outs = pl.pallas_call(
        functools.partial(keys_kernel, room, cuts),
        grid=(width // UNIT,),
        in_specs=[
            pl.BlockSpec((1, tokens), lambda i: (0, 0)),
            pl.BlockSpec((tokens, UNIT), lambda i: (0, i)),
            pl.BlockSpec((tokens, UNIT), lambda i: (0, i)),
        ],
        out_specs=[spec(room, span) for span in spans] + [spec(spare, span) for span in spare_spans],
        out_shape=[shape(room, span) for span in spans] + [shape(spare, span) for span in spare_spans],
        scratch_shapes=[pltpu.VMEM((tokens, tokens), jnp.bfloat16)],
        cost_estimate=pl.CostEstimate(
            flops=2 * tokens * tokens * width,
            bytes_accessed=6 * tokens * width,
            transcendentals=tokens * width,
        ),
        name="live_keys",
    )(token_live[None, :], gate_pre, up_pre)
    return outs[: len(widths)], outs[len(widths) :]


def gram_kernel(rows_ref, inv_ref, *refs):
    out_ref, held, sent = refs[-3:]
    slab_ref = refs[0]
    lefts = refs[1 : 1 + rows_ref.shape[0]]
    slots = held.shape[0]
    tiles = lefts[0].shape[1] // UNIT

    def leave(row, slot):
        row = pl.multiple_of(row, UNIT)
        return pltpu.make_async_copy(held.at[slot], out_ref.at[pl.ds(row, UNIT)], sent.at[slot])

    for side, left_ref in enumerate(lefts):

        def tile(i, carry, side=side, left_ref=left_ref):
            slot = lax.rem(i + side * tiles, slots)

            @pl.when(i + side * tiles >= slots)
            def _():
                leave(0, slot).wait()

            left = left_ref[:, pl.ds(pl.multiple_of(i * UNIT, UNIT), UNIT)]
            gram = lax.dot_general(
                left, slab_ref[...], (((0,), (0,)), ((), ())), preferred_element_type=jnp.float32
            )
            held[slot] = gram * inv_ref[0]
            leave(rows_ref[side] + i * UNIT, slot).start()
            return carry

        lax.fori_loop(0, tiles, tile, 0)
    for slot in range(slots):
        leave(0, slot).wait()


def gram_rows(lefts, starts, slab, inv, out, rows):
    depth, width = lefts[0].shape
    cols = slab.shape[1]
    in_specs = [pl.BlockSpec(memory_space=pltpu.SMEM)] * 2
    in_specs += [pl.BlockSpec(memory_space=pltpu.VMEM)] * (1 + len(lefts))
    operands = [jnp.stack(starts), inv, slab, *lefts]
    aliases = {}
    if out is not None:
        in_specs += [pl.BlockSpec(memory_space=pl.ANY)]
        aliases = {len(operands): 0}
        operands.append(out)
    slots = min(SLOTS, len(lefts) * width // UNIT)
    return pl.pallas_call(
        gram_kernel,
        in_specs=in_specs,
        out_specs=pl.BlockSpec(memory_space=pl.ANY),
        out_shape=jax.ShapeDtypeStruct((rows, cols), jnp.float32),
        scratch_shapes=[pltpu.VMEM((slots, UNIT, cols), jnp.float32), pltpu.SemaphoreType.DMA((slots,))],
        input_output_aliases=aliases,
        compiler_params=pltpu.CompilerParams(vmem_limit_bytes=20 << 20),
        cost_estimate=pl.CostEstimate(
            flops=2 * len(lefts) * depth * width * cols,
            bytes_accessed=4 * len(lefts) * width * cols,
            transcendentals=0,
        ),
        name="gram_rows",
    )(*operands)


def chunk_widths(width):
    units = width // UNIT
    shares = (3, 5, 4, 2)
    cuts = [units * sum(shares[:i]) // sum(shares) for i in range(len(shares) + 1)]
    return [UNIT * (cuts[i + 1] - cuts[i]) for i in range(len(shares)) if cuts[i + 1] > cuts[i]]


def pick(which, values):
    result = values[0]
    for index in range(1, len(values)):
        result = jnp.where(which == index, values[index], result)
    return result


def tied(value, *after):
    return lax.optimization_barrier((value, *after))[0]


def exchange(n_dp, n_tp, chunks, slab_here, inv):
    line = n_tp // 2
    me_dp, me_tp = lax.axis_index("dp"), lax.axis_index("tp")
    me_line, core = me_tp // 2, me_tp % 2
    count = len(chunks)
    starts = [sum(chunk.shape[1] for chunk in chunks[:i]) for i in range(count)]
    half = starts[-1] + chunks[-1].shape[1]
    rows = 2 * half * line // n_dp
    chunks = list(chunks)

    def swap_dp(value, j):
        return lax.ppermute(value, "dp", [(s, s ^ j) for s in range(n_dp)])

    def swap_core(value):
        return lax.ppermute(value, "tp", [(s, s ^ 1) for s in range(n_tp)])

    def move_line(value, target):
        return lax.ppermute(
            value, "tp", [(2 * s + c, 2 * target(s) + c) for s in range(line) for c in range(2)]
        )

    def tie(value, *stages):
        after = [part for stage in stages if stage is not None for part in stage]
        return tied(value, *after) if after else value

    direct = line // 2 + 1 if line == 4 else line
    near, held, crossed, mine, other = ({} for _ in range(5))
    out, slab = None, None
    for slot in range(count + 4):
        i = slot - 1
        if 0 <= i < count:
            held[i] = list(near[i])
            if direct < line:
                relay = jnp.where((me_line == 0) | (me_line == 3), near[i][1], near[i][2])
                held[i].append(move_line(relay, lambda s: (2, 0, 3, 1)[s]))
        i = slot
        if i < count:
            own = tie(chunks[i], near.get(i - 1), crossed.get(i - 3))
            near[i] = [own] + [move_line(own, lambda s, k=k: s ^ k) for k in range(1, direct)]
        if slot == 0:
            slabs = [slab_here] + [swap_dp(slab_here, j) for j in range(1, n_dp)]
        if slot == 1:
            slab = jnp.concatenate(slabs, axis=0)
        i = slot - 2
        if 0 <= i < count:
            picked = [pick(me_line ^ me_dp ^ j, held[i]) for j in range(n_dp)]
            if out is not None:
                picked[0], out = lax.optimization_barrier((picked[0], out))
            crossed[i] = [picked[0]] + [swap_dp(picked[j], j) for j in range(1, n_dp)]
        i = slot - 3
        if 0 <= i < count:
            mine[i] = jnp.concatenate(crossed[i], axis=0)
            other[i] = swap_core(mine[i])
        if 0 <= i < count:
            base = [side * half + starts[i] for side in (core, 1 - core)]
            if i < count - 1:
                out = gram_rows([mine[i], other[i]], base, slab, inv, out, rows)
            else:
                out = gram_rows([mine[i]], base[:1], slab, inv, out, rows)
                out = gram_rows([other[i]], base[1:], slab, inv, out, rows)
    return out


def share_rows(n_dp, n_tp, room, owns, spares, slab_offset, inv):
    kept = room - spares[0].shape[0]

    def mirror(value):
        return lax.ppermute(value, "dp", [(s, n_dp - 1 - s) for s in range(n_dp)])

    first = mirror(spares[0])
    rest = mirror(tied(spares[1], first))
    chunks, start = [], 0
    for own in owns:
        width = own.shape[1]
        extra = rest[:, start : start + width] if chunks else first
        start += width if chunks else 0
        chunks.append(jnp.concatenate([own[:kept], own[kept:] + extra], axis=0))
    slab_here = lax.dynamic_slice_in_dim(
        jnp.concatenate(chunks, axis=1), slab_offset[lax.axis_index("tp")], SLAB_DEV, 1
    )
    return exchange(n_dp, n_tp, chunks, slab_here, inv)


def all_rows(n_dp, n_tp, owns, spares, slab_offset, inv):
    chunks, start = [], 0
    for own in owns:
        width = own.shape[1]
        extra = spares[1][:, start : start + width] if chunks else spares[0]
        start += width if chunks else 0
        chunks.append(jnp.concatenate([own, extra], axis=0))
    slab_here = lax.dynamic_slice_in_dim(
        jnp.concatenate(chunks, axis=1), slab_offset[lax.axis_index("tp")], SLAB_DEV, 1
    )
    return exchange(n_dp, n_tp, chunks, slab_here, inv)


def on_device(n_dp, n_tp, gate_pre, up_pre, token_live, slab_offset):
    tokens, half = gate_pre.shape
    room = tokens * 11 // 16
    masks = [token_live] + [
        lax.ppermute(token_live, "dp", [(s, s ^ j) for s in range(n_dp)]) for j in range(1, n_dp)
    ]
    owns, spares = live_keys(gate_pre, up_pre, token_live, room, chunk_widths(half))
    tallies = [jnp.sum(mask) for mask in masks]
    inv = (1.0 / sum(tallies).astype(jnp.float32)).reshape(1)
    fits = jnp.bool_(True)
    for j in range(n_dp):
        fits &= tallies[j] + tallies[n_dp - 1 - j] <= 2 * room
    return lax.cond(
        fits,
        functools.partial(share_rows, n_dp, n_tp, room),
        functools.partial(all_rows, n_dp, n_tp),
        owns, spares, slab_offset, inv,
    )


def solution(mesh):
    placed = (P("dp", "tp"), P("dp", "tp"), P("dp"), P())
    return jax.shard_map(
        functools.partial(on_device, mesh.shape["dp"], mesh.shape["tp"]),
        mesh=mesh,
        in_specs=placed,
        out_specs=P("dp", "tp"),
        check_vma=False,
    )
```

time: 412 us -> 196 us (0.48)
  blocking collectives: 184 us -> 0 us
  waiting for transfers between devices: 137 us -> 87.2 us
  Pallas kernels: 0 us -> 43.4 us
  starting transfers between devices: 6.82 us -> 41.5 us
  matrix products: 31.8 us -> 0 us
  local copies, waits for them, and re-layouts: 29.3 us -> 6.03 us
  between operations: 16.7 us -> 5.28 us
    psum x1 -> x0, blocking collectives: 184 us -> none  [on_device(): live_total = lax.psum(jnp.sum(live_mask), 'dp')]
    all_gather x2 -> x0, waiting for transfers between devices: 137 us -> none  [the longest x1 137 us: on_device(): all_keys = lax.all_gather(key_local, 'tp', axis=1, tiled=True)]
    ppermute x0 -> x36, waiting for transfers between devices: none -> 87.2 us  [the longest x12 45.7 us: move_line(): lax.ppermute(value, 'tp', [(2 * s + c, 2 * target(s) + c) for s in range(...]
    pallas_call x0 -> x6, Pallas kernels: none -> 43.4 us  [the longest x5 32.5 us: gram_rows(): pl.pallas_call(gram_kernel, in_specs=in_specs, out_specs=pl.BlockSpec(mem...]
    ppermute x0 -> x36, starting transfers between devices: none -> 41.5 us  [the longest x15 18.2 us: swap_dp(): return lax.ppermute(value, 'dp', [(s, s ^ j) for s in range(n_dp)])]
    dot_general x1 -> x0, matrix products: 31.8 us -> none  [contract_tokens(): lax.dot_general(left, right, (((0,), (0,)), ((), ())), preferred_element_...]
    all_to_all x1 -> x0, local copies, waits for them, and re-layouts: 19.7 us -> none  [on_device(): lax.all_to_all(all_keys, 'dp', split_axis=1, concat_axis=0, tiled=True)]
    all_to_all x1 -> x0, starting transfers between devices: 6.77 us -> none  [on_device(): lax.all_to_all(all_keys, 'dp', split_axis=1, concat_axis=0, tiled=True)]
  transfers between devices with their start and end apart: 3 -> 36, of which waited for: 1 -> 14; matrix products, arithmetic and copies ran while one was open for 6% -> 7% of each run, Pallas kernels for 0% -> 20%
where the time goes in v1:
time: 196 us; the launch traced here: 195 us
  waiting for transfers between devices  87.2 us (44%)
  Pallas kernels  43.4 us (22%)
  starting transfers between devices  41.5 us (21%)
  other arithmetic  8.81 us (4%)
  local copies, waits for them, and re-layouts  6.03 us (3%)
  between operations  5.28 us (3%)
  loops' own time  2.9 us (1%)
    ppermute x12, waiting for transfers between devices, move_line(): lax.ppermute(value, 'tp', [(2 * s + c, 2 * target(s) + c) for s in range(...  45.7 us
    ppermute x15, waiting for transfers between devices, swap_dp(): return lax.ppermute(value, 'dp', [(s, s ^ j) for s in range(n_dp)])  33.7 us
    pallas_call x5, Pallas kernels, gram_rows(): pl.pallas_call(gram_kernel, in_specs=in_specs, out_specs=pl.BlockSpec(mem...  32.5 us
    ppermute x15, starting transfers between devices, swap_dp(): return lax.ppermute(value, 'dp', [(s, s ^ j) for s in range(n_dp)])  18.2 us
    ppermute x12, starting transfers between devices, move_line(): lax.ppermute(value, 'tp', [(2 * s + c, 2 * target(s) + c) for s in range(...  13.3 us
    pallas_call x1, Pallas kernels, live_keys(): pl.pallas_call(functools.partial(keys_kernel, room, cuts), grid=(width //...  10.9 us
    ppermute x2, waiting for transfers between devices, mirror(): return lax.ppermute(value, 'dp', [(s, n_dp - 1 - s) for s in range(n_dp)])  7.85 us
    ppermute x2, starting transfers between devices, mirror(): return lax.ppermute(value, 'dp', [(s, n_dp - 1 - s) for s in range(n_dp)])  5.48 us
  transfers between devices with their start and end apart: 36, of which 14 were waited for; matrix products, arithmetic and copies ran while one was open for 7% of the time, Pallas kernels for 20%

profile of v1, /device:TPU:0, one launch (start us, length us, event | category | flops | bytes accessed | tf_op | source)
XLA Modules:
  0.0 195.2 jit_solution(2454101626742328024)
XLA Ops:
  0.0 2.9 %collective-permute-start.65 = (s32[256]{0:T(256)}, s32[256]{0:T(256)S(1)}, u32[]{:S(2)}, u32[]{:S(2)}) collective-permute-start(s32[256]{0:T(256)} %param.8), channel_id=1, source_target_pairs={{0,8},{8,0},{16,24},{24,16},{1,9},{9,1},{17,25},{25,17},{2,10},{10... | collective-permute-start | bytes 3080 | tf_op jit(solution)/shard_map/ppermute | solution.py:267
  4.5 10.9 %live_keys.1 = (bf16[176,768]{1,0:T(8,128)(2,1)S(1)}, bf16[176,1280]{1,0:T(8,128)(2,1)S(1)}, bf16[176,1024]{1,0:T(8,128)(2,1)S(1)}, bf16[176,512]{1,0:T(8,128)(2...) custom-call(s32[1,256]{1,0:T(1,128)} %bitcast.20, bf16[256,3584]{1,0:T(8,128)(2,1)} %gate_ref.1, ...), custom_call_target="tpu_custom_call" | custom-call | flops 469762048 | bytes 5505024 | tf_op jit(solution)/shard_map/live_keys/pallas_call | solution.py:66
  23.0 172.0 %conditional.1 = (f32[7168,1536]{1,0:T(8,128)}) conditional(s32[]{:T(128)} %convert_element_type.6, (bf16[176,768]{1,0:T(8,128)(2,1)S(1)}, bf16[80,768]{1,0:T(8,128)(2,1)S(1)}, bf16[80,2816]{1,0:T(8,128)(2,1)}, bf16[176,1280]{1,0:T(8,128)(2,1)S(1)}, bf16[176,1024]{1,0:T(8,128)(2,1)S(1)}, /*index=5*/bf16[176,512]{1,0:T(8,128)(2,1)}, s32[8]{0:T(128)S(1)}, ...), branch_computations={%region_4.5_spmd, %region_5.6_spmd} | conditional | flops 22598254592 | bytes 194955488 | solution.py:275
  23.2 3.0 %collective-permute-start.31 = (bf16[80,768]{1,0:T(8,128)(2,1)S(1)}, bf16[80,768]{1,0:T(8,128)(2,1)S(1)}, u32[]{:S(2)}, u32[]{:S(2)}) collective-permute-start(bf16[80,768]{1,0:T(8,128)(2,1)S(1)} %get-tuple-element.57), channel_id=1, source_target_pairs={{0,24},{8,16},{16,8},{24,0},{1,25},{9,17},{17,9},{25,1},{2,26},{10... | collective-permute-start | bytes 368648 | tf_op jit(solution)/shard_map/cond/branch_1_fun/ppermute | solution.py:234
  26.2 2.9 %collective-permute-done.31 = bf16[80,768]{1,0:T(8,128)(2,1)S(1)} collective-permute-done((bf16[80,768]{1,0:T(8,128)(2,1)S(1)}, bf16[80,768]{1,0:T(8,128)(2,1)S(1)}, u32[]{:S(2)}, u32[]{:S(2)}) %collective-permute-start.31) | collective-permute-done | bytes 122912 | tf_op jit(solution)/shard_map/cond/branch_1_fun/ppermute | solution.py:234
  29.1 3.1 %collective-permute-start.37 = (bf16[176,768]{1,0:T(8,128)(2,1)S(1)}, bf16[176,768]{1,0:T(8,128)(2,1)S(1)}, u32[]{:S(2)}, u32[]{:S(2)}) collective-permute-start(bf16[176,768]{1,0:T(8,128)(2,1)S(1)} %pad_maximum_fusion.11), channel_id=1, source_target_pairs={{0,4},{1,5},{2,6},{3,7},{4,0},{5,1},{6,2},{7,3},{8,12},{9,13},{10,... | collective-permute-start | bytes 811016 | tf_op jit(solution)/shard_map/cond/branch_1_fun/ppermute | solution.py:184
  32.2 1.6 collective-permute-start.36
  35.8 1.5 slice.39
  38.8 2.5 %collective-permute-start.32 = (bf16[80,2816]{1,0:T(8,128)(2,1)S(1)}, bf16[80,2816]{1,0:T(8,128)(2,1)S(1)}, u32[]{:S(2)}, u32[]{:S(2)}) collective-permute-start(bf16[80,2816]{1,0:T(8,128)(2,1)S(1)} %copy-done.11), channel_id=1, source_target_pairs={{0,24},{8,16},{16,8},{24,0},{1,25},{9,17},{17,9},{25,1},{2,26},{10... | collective-permute-start | bytes 1351688 | tf_op jit(solution)/shard_map/cond/branch_1_fun/ppermute | solution.py:234
  44.3 5.0 %collective-permute-done.32 = bf16[80,2816]{1,0:T(8,128)(2,1)S(1)} collective-permute-done((bf16[80,2816]{1,0:T(8,128)(2,1)S(1)}, bf16[80,2816]{1,0:T(8,128)(2,1)S(1)}, u32[]{:S(2)}, u32[]{:S(2)}) %collective-permute-start.32) | collective-permute-done | bytes 450592 | tf_op jit(solution)/shard_map/cond/branch_1_fun/ppermute | solution.py:234
  51.2 20.7 %collective-permute-done.39 = bf16[176,1280]{1,0:T(8,128)(2,1)S(1)} collective-permute-done((bf16[176,1280]{1,0:T(8,128)(2,1)S(1)}, bf16[176,1280]{1,0:T(8,128)(2,1)S(1)}, u32[]{:S(2)}, u32[]{:S(2)}) %collective-permute-start.39) | collective-permute-done | bytes 450592 | tf_op jit(solution)/shard_map/cond/branch_1_fun/ppermute | solution.py:184
  72.6 3.6 %fusion.9 = bf16[176,1536]{1,0:T(8,128)(2,1)S(1)} fusion(s32[]{:T(128)S(6)} %select_n.564, bf16[96,768]{1,0:T(8,128)(2,1)S(1)} %slice.31, bf16[80,768]{1,0:T(8,128)(2,1)S(1)} %slice_add_fusion.2, bf16[96,1280]{1,0:T(8,128)(2,1)S(1)} %slice.33, bf16[80,1280]{1,0:T(8,128)(2,1)S(1)} %slice_add_fusion, bf16[96,1024]{1,0:T(8,128)(2,1)S(1)} %copy-done.3, ...), kind=kLoop, calls=%fused_computation.66 | loop fusion | flops 4325376 | bytes 1802244 | tf_op jit(solution)/shard_map/cond/branch_1_fun/concatenate | solution.py:245
  76.5 2.5 %collective-permute-start.45 = (bf16[176,768]{1,0:T(8,128)(2,1)S(1)}, bf16[176,768]{1,0:T(8,128)(2,1)S(1)}, u32[]{:S(2)}, u32[]{:S(2)}) collective-permute-start(bf16[176,768]{1,0:T(8,128)(2,1)S(1)} %get-tuple-element.108), channel_id=1, source_target_pairs={{0,24},{8,16},{16,8},{24,0},{1,25},{9,17},{17,9},{25,1},{2,26},{10... | collective-permute-start | bytes 811016 | tf_op jit(solution)/shard_map/cond/branch_1_fun/ppermute | solution.py:178
  80.1 4.2 %collective-permute-done.49 = bf16[176,1280]{1,0:T(8,128)(2,1)S(1)} collective-permute-done((bf16[176,1280]{1,0:T(8,128)(2,1)S(1)}, bf16[176,1280]{1,0:T(8,128)(2,1)S(1)}, u32[]{:S(2)}, u32[]{:S(2)}) %collective-permute-start.49) | collective-permute-done | bytes 450592 | tf_op jit(solution)/shard_map/cond/branch_1_fun/ppermute | solution.py:184
  84.5 2.5 %collective-permute-start.52 = (bf16[176,1280]{1,0:T(8,128)(2,1)S(1)}, bf16[176,1280]{1,0:T(8,128)(2,1)S(1)}, u32[]{:S(2)}, u32[]{:S(2)}) collective-permute-start(bf16[176,1280]{1,0:T(8,128)(2,1)S(1)} %get-tuple-element.101), channel_id=1, source_target_pairs={{0,24},{8,16},{16,8},{24,0},{1,25},{9,17},{17,9},{25,1},{2,26},{10... | collective-permute-start | bytes 1351688 | tf_op jit(solution)/shard_map/cond/branch_1_fun/ppermute | solution.py:178
  88.4 4.3 %collective-permute-done.44 = bf16[176,768]{1,0:T(8,128)(2,1)S(1)} collective-permute-done((bf16[176,768]{1,0:T(8,128)(2,1)S(1)}, bf16[176,768]{1,0:T(8,128)(2,1)S(1)}, u32[]{:S(2)}, u32[]{:S(2)}) %collective-permute-start.44) | collective-permute-done | bytes 270368 | tf_op jit(solution)/shard_map/cond/branch_1_fun/ppermute | solution.py:178
  92.7 1.5 collective-permute-start.51
  94.5 9.5 %collective-permute-done.41 = bf16[176,1024]{1,0:T(8,128)(2,1)S(1)} collective-permute-done((bf16[176,1024]{1,0:T(8,128)(2,1)S(1)}, bf16[176,1024]{1,0:T(8,128)(2,1)S(1)}, u32[]{:S(2)}, u32[]{:S(2)}) %collective-permute-start.41) | collective-permute-done | bytes 360480 | tf_op jit(solution)/shard_map/cond/branch_1_fun/ppermute | solution.py:184
  107.6 4.6 %collective-permute-done.51 = bf16[176,1280]{1,0:T(8,128)(2,1)S(1)} collective-permute-done((bf16[176,1280]{1,0:T(8,128)(2,1)S(1)}, bf16[176,1280]{1,0:T(8,128)(2,1)S(1)}, u32[]{:S(2)}, u32[]{:S(2)}) %collective-permute-start.51) | collective-permute-done | bytes 450592 | tf_op jit(solution)/shard_map/cond/branch_1_fun/ppermute | solution.py:178
  112.2 1.7 collective-permute-start.47
  114.0 9.7 %collective-permute-done.35 = bf16[176,1536]{1,0:T(8,128)(2,1)S(1)} collective-permute-done((bf16[176,1536]{1,0:T(8,128)(2,1)S(1)}, bf16[176,1536]{1,0:T(8,128)(2,1)S(1)}, u32[]{:S(2)}, u32[]{:S(2)}) %collective-permute-start.35) | collective-permute-done | bytes 540704 | tf_op jit(solution)/shard_map/cond/branch_1_fun/ppermute | solution.py:178
  125.1 8.5 %collective-permute-done.34 = bf16[176,1536]{1,0:T(8,128)(2,1)S(1)} collective-permute-done((bf16[176,1536]{1,0:T(8,128)(2,1)S(1)}, bf16[176,1536]{1,0:T(8,128)(2,1)S(1)}, u32[]{:S(2)}, u32[]{:S(2)}) %collective-permute-start.34) | collective-permute-done | bytes 540704 | tf_op jit(solution)/shard_map/cond/branch_1_fun/ppermute | solution.py:178
  135.2 9.8 %collective-permute-done.54 = bf16[176,1024]{1,0:T(8,128)(2,1)S(1)} collective-permute-done((bf16[176,1024]{1,0:T(8,128)(2,1)S(1)}, bf16[176,1024]{1,0:T(8,128)(2,1)S(1)}, u32[]{:S(2)}, u32[]{:S(2)}) %collective-permute-start.54) | collective-permute-done | bytes 360480 | tf_op jit(solution)/shard_map/cond/branch_1_fun/ppermute | solution.py:184
  145.1 2.5 %collective-permute-start.62 = (bf16[176,1024]{1,0:T(8,128)(2,1)S(1)}, bf16[176,1024]{1,0:T(8,128)(2,1)S(1)}, u32[]{:S(2)}, u32[]{:S(2)}) collective-permute-start(bf16[176,1024]{1,0:T(8,128)(2,1)S(1)} %get-tuple-element.104), channel_id=1, source_target_pairs={{0,24},{8,16},{16,8},{24,0},{1,25},{9,17},{17,9},{25,1},{2,26},{10... | collective-permute-start | bytes 1081352 | tf_op jit(solution)/shard_map/cond/branch_1_fun/ppermute | solution.py:178
  148.7 6.5 %gram_rows.15.refs_3_ = f32[7168,1536]{1,0:T(8,128)} custom-call(s32[2]{0:T(128)S(1)} %pad_add_fusion.4.rows_ref, f32[1]{0:T(128)} %get-tuple-element.55.inv_ref, bf16[704,1536]{1,0:T(8,128)(2,1)S(1)} %pad_maximum_fusion.6.refs_0_, bf16[704,768]{1,0:T(8,128)(2,1)S(1)} %pad_maximum_fusion.8.refs_1_, bf16[704,768]{1,0:T(8,128)(2,1)S(1)} %collective-permute-done.55.refs_2_), custom_call_target="tpu_custom_call" | custom-call | flops 3321888768 | bytes 9437184 | tf_op jit(solution)/shard_map/cond/branch_1_fun/gram_rows/pallas_call | solution.py:132
  156.0 6.4 %collective-permute-done.60 = bf16[176,1024]{1,0:T(8,128)(2,1)S(1)} collective-permute-done((bf16[176,1024]{1,0:T(8,128)(2,1)S(1)}, bf16[176,1024]{1,0:T(8,128)(2,1)S(1)}, u32[]{:S(2)}, u32[]{:S(2)}) %collective-permute-start.60) | collective-permute-done | bytes 360480 | tf_op jit(solution)/shard_map/cond/branch_1_fun/ppermute | solution.py:178
  164.8 1.5 collective-permute-start.58
  166.3 1.6 collective-permute-start.57
  168.4 9.8 %gram_rows.16.refs_3_ = f32[7168,1536]{1,0:T(8,128)} custom-call(s32[2]{0:T(128)S(1)} %pad_add_fusion.3.rows_ref, f32[1]{0:T(128)} %get-tuple-element.55.inv_ref, bf16[704,1536]{1,0:T(8,128)(2,1)S(1)} %pad_maximum_fusion.6.refs_0_, bf16[704,1280]{1,0:T(8,128)(2,1)S(1)} %pad_maximum_fusion.7.refs_1_, ...), custom_call_target="tpu_custom_call", output_to_operand_aliasing={{}: (5, {})} | custom-call | flops 5536481280 | bytes 15728640 | tf_op jit(solution)/shard_map/cond/branch_1_fun/gram_rows/pallas_call | solution.py:132
  178.4 9.5 %gram_rows.17.refs_2_ = f32[7168,1536]{1,0:T(8,128)} custom-call(s32[2]{0:T(128)S(1)} %pad_add_fusion.5.rows_ref, f32[1]{0:T(128)} %get-tuple-element.55.inv_ref, bf16[704,1536]{1,0:T(8,128)(2,1)S(1)} %pad_maximum_fusion.6.refs_0_, bf16[704,1024]{1,0:T(8,128)(2,1)} %constant_dynamic-update-slice_fusion.14.refs_1_, ...), custom_call_target="tpu_custom_call", output_to_operand_aliasing={{}: (5, {})} | custom-call | flops 4429185024 | bytes 12582912 | tf_op jit(solution)/shard_map/cond/branch_1_fun/gram_rows/pallas_call | solution.py:132
  188.0 2.8 %gram_rows.18.refs_2_ = f32[7168,1536]{1,0:T(8,128)} custom-call(s32[1]{0:T(128)} %bitcast.15.rows_ref, f32[1]{0:T(128)} %get-tuple-element.55.inv_ref, bf16[704,1536]{1,0:T(8,128)(2,1)S(1)} %pad_maximum_fusion.6.refs_0_, bf16[704,512]{1,0:T(8,128)(2,1)S(1)} %constant_dynamic-update-slice_fusion.10.refs_1_, ...), custom_call_target="tpu_custom_call", output_to_operand_aliasing={{}: (4, {})} | custom-call | flops 1107296256 | bytes 3145728 | tf_op jit(solution)/shard_map/cond/branch_1_fun/gram_rows/pallas_call | solution.py:132
  190.8 3.9 %gram_rows.19 = f32[7168,1536]{1,0:T(8,128)} custom-call(s32[1]{0:T(128)} %bitcast.9.rows_ref, f32[1]{0:T(128)} %get-tuple-element.55.inv_ref, bf16[704,1536]{1,0:T(8,128)(2,1)S(1)} %pad_maximum_fusion.6.refs_0_, bf16[704,512]{1,0:T(8,128)(2,1)} %collective-permute-done.59.refs_1_, f32[7168,1536]{1,0:T(8,128)} %gram_rows.18.refs_2_), custom_call_target="tpu_custom_call", output_to_operand_aliasing={{}: (4, {})} | custom-call | flops 1107296256 | bytes 3145728 | tf_op jit(solution)/shard_map/cond/branch_1_fun/gram_rows/pallas_call | solution.py:132
  (98 shorter events, 25.8 us)
Async XLA Ops:
  0.0 16.0 %collective-permute-start.65 = (s32[256]{0:T(256)}, s32[256]{0:T(256)S(1)}, u32[]{:S(2)}, u32[]{:S(2)}) collective-permute-start(s32[256]{0:T(256)} %param.8), channel_id=1, source_target_pairs={{0,8},{8,0},{16,24},{24,16},{1,9},{9,1},{17,25},{25,17},{2,10},{10... | collective-permute-start | bytes 3080 | tf_op jit(solution)/shard_map/ppermute | solution.py:267
  2.9 14.9 %collective-permute-start.64 = (s32[256]{0:T(256)}, s32[256]{0:T(256)S(1)}, u32[]{:S(2)}, u32[]{:S(2)}) collective-permute-start(s32[256]{0:T(256)} %param.8), channel_id=1, source_target_pairs={{0,24},{8,16},{16,8},{24,0},{1,25},{9,17},{17,9},{25,1},{2,26},{10... | collective-permute-start | bytes 3080 | tf_op jit(solution)/shard_map/ppermute | solution.py:267
  4.4 15.3 %collective-permute-start.66 = (s32[256]{0:T(256)}, s32[256]{0:T(256)S(1)}, u32[]{:S(2)}, u32[]{:S(2)}) collective-permute-start(s32[256]{0:T(256)} %param.8), channel_id=1, source_target_pairs={{0,16},{8,24},{16,0},{24,8},{1,17},{9,25},{17,1},{25,9},{2,18},{10... | collective-permute-start | bytes 3080 | tf_op jit(solution)/shard_map/ppermute | solution.py:267
  29.1 13.5 %collective-permute-start.37 = (bf16[176,768]{1,0:T(8,128)(2,1)S(1)}, bf16[176,768]{1,0:T(8,128)(2,1)S(1)}, u32[]{:S(2)}, u32[]{:S(2)}) collective-permute-start(bf16[176,768]{1,0:T(8,128)(2,1)S(1)} %pad_maximum_fusion.11), channel_id=1, source_target_pairs={{0,4},{1,5},{2,6},{3,7},{4,0},{5,1},{6,2},{7,3},{8,12},{9,13},{10,... | collective-permute-start | bytes 811016 | tf_op jit(solution)/shard_map/cond/branch_1_fun/ppermute | solution.py:184
  42.9 33.4 %collective-permute-start.42 = (bf16[176,768]{1,0:T(8,128)(2,1)S(1)}, bf16[176,768]{1,0:T(8,128)(2,1)S(1)}, u32[]{:S(2)}, u32[]{:S(2)}) collective-permute-start(bf16[176,768]{1,0:T(8,128)(2,1)S(1)} %broadcast_select_fusion.6), channel_id=1, source_target_pairs={{0,4},{1,5},{2,0},{3,1},{4,6},{5,7},{6,2},{7,3},{8,12},{9,13},{10,... | collective-permute-start | bytes 811016 | tf_op jit(solution)/shard_map/cond/branch_1_fun/ppermute | solution.py:184
  49.3 22.6 %collective-permute-start.39 = (bf16[176,1280]{1,0:T(8,128)(2,1)S(1)}, bf16[176,1280]{1,0:T(8,128)(2,1)S(1)}, u32[]{:S(2)}, u32[]{:S(2)}) collective-permute-start(bf16[176,1280]{1,0:T(8,128)(2,1)S(1)} %pad_maximum_fusion.9), channel_id=1, source_target_pairs={{0,4},{1,5},{2,6},{3,7},{4,0},{5,1},{6,2},{7,3},{8,12},{9,13},{10,... | collective-permute-start | bytes 1351688 | tf_op jit(solution)/shard_map/cond/branch_1_fun/ppermute | solution.py:184
  49.8 22.1 %collective-permute-start.38 = (bf16[176,1280]{1,0:T(8,128)(2,1)S(1)}, bf16[176,1280]{1,0:T(8,128)(2,1)S(1)}, u32[]{:S(2)}, u32[]{:S(2)}) collective-permute-start(bf16[176,1280]{1,0:T(8,128)(2,1)S(1)} %pad_maximum_fusion.9), channel_id=1, source_target_pairs={{0,2},{1,3},{2,0},{3,1},{4,6},{5,7},{6,4},{7,5},{8,10},{9,11},{10,... | collective-permute-start | bytes 1351688 | tf_op jit(solution)/shard_map/cond/branch_1_fun/ppermute | solution.py:184
  72.0 12.3 %collective-permute-start.49 = (bf16[176,1280]{1,0:T(8,128)(2,1)S(1)}, bf16[176,1280]{1,0:T(8,128)(2,1)S(1)}, u32[]{:S(2)}, u32[]{:S(2)}) collective-permute-start(bf16[176,1280]{1,0:T(8,128)(2,1)S(1)} %broadcast_select_fusion.4), channel_id=1, source_target_pairs={{0,4},{1,5},{2,0},{3,1},{4,6},{5,7},{6,2},{7,3},{8,12},{9,13},{10,... | collective-permute-start | bytes 1351688 | tf_op jit(solution)/shard_map/cond/branch_1_fun/ppermute | solution.py:184
  76.5 11.7 %collective-permute-start.45 = (bf16[176,768]{1,0:T(8,128)(2,1)S(1)}, bf16[176,768]{1,0:T(8,128)(2,1)S(1)}, u32[]{:S(2)}, u32[]{:S(2)}) collective-permute-start(bf16[176,768]{1,0:T(8,128)(2,1)S(1)} %get-tuple-element.108), channel_id=1, source_target_pairs={{0,24},{8,16},{16,8},{24,0},{1,25},{9,17},{17,9},{25,1},{2,26},{10... | collective-permute-start | bytes 811016 | tf_op jit(solution)/shard_map/cond/branch_1_fun/ppermute | solution.py:178
  79.0 13.6 %collective-permute-start.44 = (bf16[176,768]{1,0:T(8,128)(2,1)S(1)}, bf16[176,768]{1,0:T(8,128)(2,1)S(1)}, u32[]{:S(2)}, u32[]{:S(2)}) collective-permute-start(bf16[176,768]{1,0:T(8,128)(2,1)S(1)} %get-tuple-element.109), channel_id=1, source_target_pairs={{0,16},{8,24},{16,0},{24,8},{1,17},{9,25},{17,1},{25,9},{2,18},{10... | collective-permute-start | bytes 811016 | tf_op jit(solution)/shard_map/cond/branch_1_fun/ppermute | solution.py:178
  79.6 14.6 %collective-permute-start.43 = (bf16[176,768]{1,0:T(8,128)(2,1)S(1)}, bf16[176,768]{1,0:T(8,128)(2,1)S(1)}, u32[]{:S(2)}, u32[]{:S(2)}) collective-permute-start(bf16[176,768]{1,0:T(8,128)(2,1)S(1)} %get-tuple-element.110), channel_id=1, source_target_pairs={{0,8},{8,0},{16,24},{24,16},{1,9},{9,1},{17,25},{25,17},{2,10},{10... | collective-permute-start | bytes 811016 | tf_op jit(solution)/shard_map/cond/branch_1_fun/ppermute | solution.py:178
  84.5 21.5 %collective-permute-start.52 = (bf16[176,1280]{1,0:T(8,128)(2,1)S(1)}, bf16[176,1280]{1,0:T(8,128)(2,1)S(1)}, u32[]{:S(2)}, u32[]{:S(2)}) collective-permute-start(bf16[176,1280]{1,0:T(8,128)(2,1)S(1)} %get-tuple-element.101), channel_id=1, source_target_pairs={{0,24},{8,16},{16,8},{24,0},{1,25},{9,17},{17,9},{25,1},{2,26},{10... | collective-permute-start | bytes 1351688 | tf_op jit(solution)/shard_map/cond/branch_1_fun/ppermute | solution.py:178
  87.0 17.0 %collective-permute-start.41 = (bf16[176,1024]{1,0:T(8,128)(2,1)S(1)}, bf16[176,1024]{1,0:T(8,128)(2,1)S(1)}, u32[]{:S(2)}, u32[]{:S(2)}) collective-permute-start(bf16[176,1024]{1,0:T(8,128)(2,1)S(1)} %pad_maximum_fusion.10), channel_id=1, source_target_pairs={{0,4},{1,5},{2,6},{3,7},{4,0},{5,1},{6,2},{7,3},{8,12},{9,13},{10,... | collective-permute-start | bytes 1081352 | tf_op jit(solution)/shard_map/cond/branch_1_fun/ppermute | solution.py:184
  88.3 16.3 %collective-permute-start.40 = (bf16[176,1024]{1,0:T(8,128)(2,1)S(1)}, bf16[176,1024]{1,0:T(8,128)(2,1)S(1)}, u32[]{:S(2)}, u32[]{:S(2)}) collective-permute-start(bf16[176,1024]{1,0:T(8,128)(2,1)S(1)} %pad_maximum_fusion.10), channel_id=1, source_target_pairs={{0,2},{1,3},{2,0},{3,1},{4,6},{5,7},{6,4},{7,5},{8,10},{9,11},{10,... | collective-permute-start | bytes 1081352 | tf_op jit(solution)/shard_map/cond/branch_1_fun/ppermute | solution.py:184
  92.7 19.5 %collective-permute-start.51 = (bf16[176,1280]{1,0:T(8,128)(2,1)S(1)}, bf16[176,1280]{1,0:T(8,128)(2,1)S(1)}, u32[]{:S(2)}, u32[]{:S(2)}) collective-permute-start(bf16[176,1280]{1,0:T(8,128)(2,1)S(1)} %get-tuple-element.102), channel_id=1, source_target_pairs={{0,16},{8,24},{16,0},{24,8},{1,17},{9,25},{17,1},{25,9},{2,18},{10... | collective-permute-start | bytes 1351688 | tf_op jit(solution)/shard_map/cond/branch_1_fun/ppermute | solution.py:178
  94.2 18.0 %collective-permute-start.50 = (bf16[176,1280]{1,0:T(8,128)(2,1)S(1)}, bf16[176,1280]{1,0:T(8,128)(2,1)S(1)}, u32[]{:S(2)}, u32[]{:S(2)}) collective-permute-start(bf16[176,1280]{1,0:T(8,128)(2,1)S(1)} %get-tuple-element.103), channel_id=1, source_target_pairs={{0,8},{8,0},{16,24},{24,16},{1,9},{9,1},{17,25},{25,17},{2,10},{10... | collective-permute-start | bytes 1351688 | tf_op jit(solution)/shard_map/cond/branch_1_fun/ppermute | solution.py:178
  104.0 19.7 %collective-permute-start.35 = (bf16[176,1536]{1,0:T(8,128)(2,1)S(1)}, bf16[176,1536]{1,0:T(8,128)(2,1)S(1)}, u32[]{:S(2)}, u32[]{:S(2)}) collective-permute-start(bf16[176,1536]{1,0:T(8,128)(2,1)S(1)} %fusion.9), channel_id=1, source_target_pairs={{0,24},{8,16},{16,8},{24,0},{1,25},{9,17},{17,9},{25,1},{2,26},{10... | collective-permute-start | bytes 1622024 | tf_op jit(solution)/shard_map/cond/branch_1_fun/ppermute | solution.py:178
  104.6 29.1 %collective-permute-start.34 = (bf16[176,1536]{1,0:T(8,128)(2,1)S(1)}, bf16[176,1536]{1,0:T(8,128)(2,1)S(1)}, u32[]{:S(2)}, u32[]{:S(2)}) collective-permute-start(bf16[176,1536]{1,0:T(8,128)(2,1)S(1)} %fusion.9), channel_id=1, source_target_pairs={{0,16},{8,24},{16,0},{24,8},{1,17},{9,25},{17,1},{25,9},{2,18},{10... | collective-permute-start | bytes 1622024 | tf_op jit(solution)/shard_map/cond/branch_1_fun/ppermute | solution.py:178
  106.0 28.3 %collective-permute-start.33 = (bf16[176,1536]{1,0:T(8,128)(2,1)S(1)}, bf16[176,1536]{1,0:T(8,128)(2,1)S(1)}, u32[]{:S(2)}, u32[]{:S(2)}) collective-permute-start(bf16[176,1536]{1,0:T(8,128)(2,1)S(1)} %fusion.9), channel_id=1, source_target_pairs={{0,8},{8,0},{16,24},{24,16},{1,9},{9,1},{17,25},{25,17},{2,10},{10... | collective-permute-start | bytes 1622024 | tf_op jit(solution)/shard_map/cond/branch_1_fun/ppermute | solution.py:178
  112.2 36.0 %collective-permute-start.55 = (bf16[704,768]{1,0:T(8,128)(2,1)S(1)}, bf16[704,768]{1,0:T(8,128)(2,1)S(1)}, u32[]{:S(2)}, u32[]{:S(2)}) collective-permute-start(bf16[704,768]{1,0:T(8,128)(2,1)S(1)} %pad_maximum_fusion.8.refs_1_), channel_id=1, source_target_pairs={{0,1},{1,0},{2,3},{3,2},{4,5},{5,4},{6,7},{7,6},{8,9},{9,8},{10,11... | collective-permute-start | bytes 3244040 | tf_op jit(solution)/shard_map/cond/branch_1_fun/ppermute | solution.py:181
  112.2 22.3 %collective-permute-start.47 = (bf16[176,512]{1,0:T(8,128)(2,1)S(1)}, bf16[176,512]{1,0:T(8,128)(2,1)S(1)}, u32[]{:S(2)}, u32[]{:S(2)}) collective-permute-start(bf16[176,512]{1,0:T(8,128)(2,1)S(1)} %pad_maximum_fusion.12), channel_id=1, source_target_pairs={{0,4},{1,5},{2,6},{3,7},{4,0},{5,1},{6,2},{7,3},{8,12},{9,13},{10,... | collective-permute-start | bytes 540680 | tf_op jit(solution)/shard_map/cond/branch_1_fun/ppermute | solution.py:184
  123.7 10.8 %collective-permute-start.46 = (bf16[176,512]{1,0:T(8,128)(2,1)S(1)}, bf16[176,512]{1,0:T(8,128)(2,1)S(1)}, u32[]{:S(2)}, u32[]{:S(2)}) collective-permute-start(bf16[176,512]{1,0:T(8,128)(2,1)S(1)} %pad_maximum_fusion.12), channel_id=1, source_target_pairs={{0,2},{1,3},{2,0},{3,1},{4,6},{5,7},{6,4},{7,5},{8,10},{9,11},{10,... | collective-permute-start | bytes 540680 | tf_op jit(solution)/shard_map/cond/branch_1_fun/ppermute | solution.py:184
  133.7 11.3 %collective-permute-start.54 = (bf16[176,1024]{1,0:T(8,128)(2,1)S(1)}, bf16[176,1024]{1,0:T(8,128)(2,1)S(1)}, u32[]{:S(2)}, u32[]{:S(2)}) collective-permute-start(bf16[176,1024]{1,0:T(8,128)(2,1)S(1)} %broadcast_select_fusion.5), channel_id=1, source_target_pairs={{0,4},{1,5},{2,0},{3,1},{4,6},{5,7},{6,2},{7,3},{8,12},{9,13},{10,... | collective-permute-start | bytes 1081352 | tf_op jit(solution)/shard_map/cond/branch_1_fun/ppermute | solution.py:184
  134.3 34.0 %collective-permute-start.53 = (bf16[704,1280]{1,0:T(8,128)(2,1)S(1)}, bf16[704,1280]{1,0:T(8,128)(2,1)S(1)}, u32[]{:S(2)}, u32[]{:S(2)}) collective-permute-start(bf16[704,1280]{1,0:T(8,128)(2,1)S(1)} %pad_maximum_fusion.7.refs_1_), channel_id=1, source_target_pairs={{0,1},{1,0},{2,3},{3,2},{4,5},{5,4},{6,7},{7,6},{8,9},{9,8},{10,11... | collective-permute-start | bytes 5406728 | tf_op jit(solution)/shard_map/cond/branch_1_fun/ppermute | solution.py:181
  134.5 30.2 %collective-permute-start.48 = (bf16[176,512]{1,0:T(8,128)(2,1)S(1)}, bf16[176,512]{1,0:T(8,128)(2,1)S(1)}, u32[]{:S(2)}, u32[]{:S(2)}) collective-permute-start(bf16[176,512]{1,0:T(8,128)(2,1)S(1)} %broadcast_select_fusion.7), channel_id=1, source_target_pairs={{0,4},{1,5},{2,0},{3,1},{4,6},{5,7},{6,2},{7,3},{8,12},{9,13},{10,... | collective-permute-start | bytes 540680 | tf_op jit(solution)/shard_map/cond/branch_1_fun/ppermute | solution.py:184
  145.1 18.9 %collective-permute-start.62 = (bf16[176,1024]{1,0:T(8,128)(2,1)S(1)}, bf16[176,1024]{1,0:T(8,128)(2,1)S(1)}, u32[]{:S(2)}, u32[]{:S(2)}) collective-permute-start(bf16[176,1024]{1,0:T(8,128)(2,1)S(1)} %get-tuple-element.104), channel_id=1, source_target_pairs={{0,24},{8,16},{16,8},{24,0},{1,25},{9,17},{17,9},{25,1},{2,26},{10... | collective-permute-start | bytes 1081352 | tf_op jit(solution)/shard_map/cond/branch_1_fun/ppermute | solution.py:178
  147.6 15.6 %collective-permute-start.61 = (bf16[176,1024]{1,0:T(8,128)(2,1)S(1)}, bf16[176,1024]{1,0:T(8,128)(2,1)S(1)}, u32[]{:S(2)}, u32[]{:S(2)}) collective-permute-start(bf16[176,1024]{1,0:T(8,128)(2,1)S(1)} %get-tuple-element.105), channel_id=1, source_target_pairs={{0,16},{8,24},{16,0},{24,8},{1,17},{9,25},{17,1},{25,9},{2,18},{10... | collective-permute-start | bytes 1081352 | tf_op jit(solution)/shard_map/cond/branch_1_fun/ppermute | solution.py:178
  148.1 14.3 %collective-permute-start.60 = (bf16[176,1024]{1,0:T(8,128)(2,1)S(1)}, bf16[176,1024]{1,0:T(8,128)(2,1)S(1)}, u32[]{:S(2)}, u32[]{:S(2)}) collective-permute-start(bf16[176,1024]{1,0:T(8,128)(2,1)S(1)} %get-tuple-element.106), channel_id=1, source_target_pairs={{0,8},{8,0},{16,24},{24,16},{1,9},{9,1},{17,25},{25,17},{2,10},{10... | collective-permute-start | bytes 1081352 | tf_op jit(solution)/shard_map/cond/branch_1_fun/ppermute | solution.py:178
  164.7 13.7 %collective-permute-start.63 = (bf16[704,1024]{1,0:T(8,128)(2,1)}, bf16[704,1024]{1,0:T(8,128)(2,1)}, u32[]{:S(2)}, u32[]{:S(2)}) collective-permute-start(bf16[704,1024]{1,0:T(8,128)(2,1)} %constant_dynamic-update-slice_fusion.14.refs_1_), channel_id=1, source_target_pairs={{0,1},{1,0},{2,3},{3,2},{4,5},{5,4},{6,7},{7,6},{8,9},{9,8},{10,11... | collective-permute-start | bytes 4325384 | tf_op jit(solution)/shard_map/cond/branch_1_fun/ppermute | solution.py:181
  164.8 13.4 %collective-permute-start.58 = (bf16[176,512]{1,0:T(8,128)(2,1)S(1)}, bf16[176,512]{1,0:T(8,128)(2,1)S(1)}, u32[]{:S(2)}, u32[]{:S(2)}) collective-permute-start(bf16[176,512]{1,0:T(8,128)(2,1)S(1)} %get-tuple-element.111), channel_id=1, source_target_pairs={{0,24},{8,16},{16,8},{24,0},{1,25},{9,17},{17,9},{25,1},{2,26},{10... | collective-permute-start | bytes 540680 | tf_op jit(solution)/shard_map/cond/branch_1_fun/ppermute | solution.py:178
  166.3 11.9 %collective-permute-start.57 = (bf16[176,512]{1,0:T(8,128)(2,1)S(1)}, bf16[176,512]{1,0:T(8,128)(2,1)S(1)}, u32[]{:S(2)}, u32[]{:S(2)}) collective-permute-start(bf16[176,512]{1,0:T(8,128)(2,1)S(1)} %get-tuple-element.112), channel_id=1, source_target_pairs={{0,16},{8,24},{16,0},{24,8},{1,17},{9,25},{17,1},{25,9},{2,18},{10... | collective-permute-start | bytes 540680 | tf_op jit(solution)/shard_map/cond/branch_1_fun/ppermute | solution.py:178
  178.3 12.5 %collective-permute-start.59 = (bf16[704,512]{1,0:T(8,128)(2,1)S(1)}, bf16[704,512]{1,0:T(8,128)(2,1)}, u32[]{:S(2)}, u32[]{:S(2)}) collective-permute-start(bf16[704,512]{1,0:T(8,128)(2,1)S(1)} %constant_dynamic-update-slice_fusion.10.refs_1_), channel_id=1, source_target_pairs={{0,1},{1,0},{2,3},{3,2},{4,5},{5,4},{6,7},{7,6},{8,9},{9,8},{10,11... | collective-permute-start | bytes 2162696 | tf_op jit(solution)/shard_map/cond/branch_1_fun/ppermute | solution.py:181
  (9 other events, 132.4 us)

commit v2 on v0

v2 whole, which is shorter than its diff:
```python
import functools

import jax
import jax.numpy as jnp
from jax import lax
from jax.experimental import pallas as pl
from jax.experimental.pallas import tpu as pltpu
from jax.sharding import PartitionSpec as P

SLAB_DEV = 1536
UNIT = 256
SLOTS = 4
SHARES = (4, 4, 4, 2)


def keys_kernel(room, widths, live_ref, gate_ref, up_ref, *refs):
    own_refs, spare_refs = refs[: len(widths)], refs[len(widths) :]
    tokens = gate_ref.shape[0]
    live = live_ref[...].astype(jnp.float32)
    slot_id = lax.broadcasted_iota(jnp.int32, (tokens, tokens), 0)
    token_id = lax.broadcasted_iota(jnp.int32, (tokens, tokens), 1)
    upto = (slot_id <= token_id).astype(jnp.float32)
    rank = (jnp.dot(jnp.broadcast_to(live, (8, tokens)), upto, preferred_element_type=jnp.float32) - 1.0)[:1]
    slot = jnp.where(rank < room, rank, tokens - jnp.sum(live) + rank)
    order = ((slot_id.astype(jnp.float32) == slot) & (live > 0)).astype(jnp.bfloat16)

    def place(columns):
        gate = gate_ref[:, columns].astype(jnp.float32)
        key = (0.5 * gate) * (1.0 + jnp.tanh(0.5 * gate)) * up_ref[:, columns].astype(jnp.float32)
        return jnp.dot(order, key.astype(jnp.bfloat16), preferred_element_type=jnp.float32).astype(jnp.bfloat16)

    for c, width in enumerate(widths):
        start = sum(widths[:c])
        shift = start - widths[0] if c else 0

        def fill(i, carry, c=c, start=start, shift=shift):
            at = pl.multiple_of(i * UNIT, UNIT)
            placed = place(pl.ds(start + at, UNIT))
            own_refs[c][:, pl.ds(at, UNIT)] = placed[:room]
            spare_refs[min(c, 1)][:, pl.ds(shift + at, UNIT)] = placed[room:]
            return carry

        lax.fori_loop(0, width // UNIT, fill, 0)


def live_keys(gate_pre, up_pre, token_live, room, widths):
    tokens, width = gate_pre.shape
    spare = tokens - room
    shapes = [(room, part) for part in widths] + [(spare, widths[0]), (spare, width - widths[0])]
    outs = pl.pallas_call(
        functools.partial(keys_kernel, room, widths),
        in_specs=[pl.BlockSpec(memory_space=pltpu.VMEM)] * 3,
        out_specs=[pl.BlockSpec(memory_space=pltpu.VMEM)] * len(shapes),
        out_shape=[jax.ShapeDtypeStruct(shape, jnp.bfloat16) for shape in shapes],
        compiler_params=pltpu.CompilerParams(vmem_limit_bytes=12 << 20),
        cost_estimate=pl.CostEstimate(
            flops=2 * tokens * tokens * width,
            bytes_accessed=6 * tokens * width,
            transcendentals=tokens * width,
        ),
        name="live_keys",
    )(token_live, gate_pre, up_pre)
    return outs[: len(widths)], outs[len(widths) :]


def join_kernel(*refs):
    parts, out_ref = refs[:-1], refs[-1]
    rows = parts[0].shape[0]
    for i, part in enumerate(parts):
        out_ref[i * rows : (i + 1) * rows, :] = part[...]


def joined(parts):
    rows, cols = parts[0].shape
    return pl.pallas_call(
        join_kernel,
        in_specs=[pl.BlockSpec(memory_space=pltpu.VMEM)] * len(parts),
        out_specs=pl.BlockSpec(memory_space=pltpu.VMEM),
        out_shape=jax.ShapeDtypeStruct((len(parts) * rows, cols), parts[0].dtype),
        compiler_params=pltpu.CompilerParams(vmem_limit_bytes=8 << 20),
        cost_estimate=pl.CostEstimate(flops=0, bytes_accessed=1 << 20, transcendentals=0),
        name="joined",
    )(*parts)


def deal_kernel(which_ref, *refs):
    count = len(refs) // 2
    for which in range(count):

        @pl.when(which_ref[0] == which)
        def _(which=which):
            for j in range(count):
                refs[count + j][...] = refs[j ^ which][...]


def dealt(which, values):
    return pl.pallas_call(
        deal_kernel,
        in_specs=[pl.BlockSpec(memory_space=pltpu.SMEM)] + [pl.BlockSpec(memory_space=pltpu.VMEM)] * len(values),
        out_specs=[pl.BlockSpec(memory_space=pltpu.VMEM)] * len(values),
        out_shape=[jax.ShapeDtypeStruct(value.shape, value.dtype) for value in values],
        compiler_params=pltpu.CompilerParams(vmem_limit_bytes=8 << 20),
        cost_estimate=pl.CostEstimate(flops=0, bytes_accessed=1 << 20, transcendentals=0),
        name="dealt",
    )(which, *values)


def gram_kernel(rows_ref, total_ref, *refs):
    out_ref, held, sent = refs[-3:]
    slab_ref = refs[0]
    lefts = refs[1 : 1 + rows_ref.shape[0]]
    slots = held.shape[0]
    tiles = lefts[0].shape[1] // UNIT
    inv = 1.0 / jnp.full((1, held.shape[2]), total_ref[0], jnp.float32)

    def leave(row, slot):
        row = pl.multiple_of(row, UNIT)
        return pltpu.make_async_copy(held.at[slot], out_ref.at[pl.ds(row, UNIT)], sent.at[slot])

    for side, left_ref in enumerate(lefts):

        def tile(i, carry, side=side, left_ref=left_ref):
            slot = lax.rem(i + side * tiles, slots)

            @pl.when(i + side * tiles >= slots)
            def _():
                leave(0, slot).wait()

            left = left_ref[:, pl.ds(pl.multiple_of(i * UNIT, UNIT), UNIT)]
            gram = lax.dot_general(
                left, slab_ref[...], (((0,), (0,)), ((), ())), preferred_element_type=jnp.float32
            )
            held[slot] = gram * inv
            leave(rows_ref[side] + i * UNIT, slot).start()
            return carry

        lax.fori_loop(0, tiles, tile, 0)
    for slot in range(slots):
        leave(0, slot).wait()


def gram_rows(lefts, starts, slab, total, out, rows):
    depth, width = lefts[0].shape
    cols = slab.shape[1]
    in_specs = [pl.BlockSpec(memory_space=pltpu.SMEM)] * 2
    in_specs += [pl.BlockSpec(memory_space=pltpu.VMEM)] * (1 + len(lefts))
    operands = [jnp.stack(starts), total, slab, *lefts]
    aliases = {}
    if out is not None:
        in_specs += [pl.BlockSpec(memory_space=pl.ANY)]
        aliases = {len(operands): 0}
        operands.append(out)
    slots = min(SLOTS, len(lefts) * width // UNIT)
    return pl.pallas_call(
        gram_kernel,
        in_specs=in_specs,
        out_specs=pl.BlockSpec(memory_space=pl.ANY),
        out_shape=jax.ShapeDtypeStruct((rows, cols), jnp.float32),
        scratch_shapes=[pltpu.VMEM((slots, UNIT, cols), jnp.float32), pltpu.SemaphoreType.DMA((slots,))],
        input_output_aliases=aliases,
        compiler_params=pltpu.CompilerParams(vmem_limit_bytes=20 << 20),
        cost_estimate=pl.CostEstimate(
            flops=2 * len(lefts) * depth * width * cols,
            bytes_accessed=4 * len(lefts) * width * cols,
            transcendentals=0,
        ),
        name="gram_rows",
    )(*operands)


def chunk_widths(width):
    units = width // UNIT
    shares = SHARES
    cuts = [units * sum(shares[:i]) // sum(shares) for i in range(len(shares) + 1)]
    return [UNIT * (cuts[i + 1] - cuts[i]) for i in range(len(shares)) if cuts[i + 1] > cuts[i]]


def tally_kernel(room, *refs):
    masks, total_ref, fits_ref = refs[:-2], refs[-2], refs[-1]
    tallies = [jnp.sum(ref[...].astype(jnp.float32)) for ref in masks]
    total_ref[0] = sum(tallies)
    fits = tallies[0] + tallies[-1] <= 2.0 * room
    for j in range(1, len(masks) // 2):
        fits &= tallies[j] + tallies[len(masks) - 1 - j] <= 2.0 * room
    fits_ref[0] = fits.astype(jnp.int32)


def tally(masks, room):
    return pl.pallas_call(
        functools.partial(tally_kernel, room),
        in_specs=[pl.BlockSpec(memory_space=pltpu.VMEM)] * len(masks),
        out_specs=[pl.BlockSpec(memory_space=pltpu.SMEM)] * 2,
        out_shape=[jax.ShapeDtypeStruct((1,), jnp.float32), jax.ShapeDtypeStruct((1,), jnp.int32)],
        name="tally",
    )(*masks)


def tied(value, *after):
    return lax.optimization_barrier((value, *after))[0]


def exchange(n_dp, n_tp, widths, first_chunk, later, slab_offset, total):
    line = n_tp // 2
    me_dp, me_tp = lax.axis_index("dp"), lax.axis_index("tp")
    me_line, core = me_tp // 2, me_tp % 2
    count = len(widths)
    starts = [sum(widths[:i]) for i in range(count)]
    half = sum(widths)
    rows = 2 * half * line // n_dp

    def swap_dp(value, j):
        return lax.ppermute(value, "dp", [(s, s ^ j) for s in range(n_dp)])

    def swap_core(value):
        return lax.ppermute(value, "tp", [(s, s ^ 1) for s in range(n_tp)])

    def move_line(value, target):
        return lax.ppermute(
            value, "tp", [(2 * s + c, 2 * target(s) + c) for s in range(line) for c in range(2)]
        )

    direct = line // 2 + 1 if line == 4 else line

    def spread(own):
        return [own] + [move_line(own, lambda s, k=k: s ^ k) for k in range(1, direct)]

    def grams(i, sides, mine, other, out):
        lefts = [(mine, other)[side] for side in sides]
        places = [(core, 1 - core)[side] * half + starts[i] for side in sides]
        return gram_rows(lefts, places, slab, total, out, rows)

    which = (me_line ^ me_dp).astype(jnp.int32).reshape(1)
    near = {0: spread(first_chunk)}
    late, merge = later()
    held, crossed = {}, {}
    chunks, out, slab, slabs = {}, None, None, None
    for slot in range(1, count + 3):
        near, held, crossed, chunks, late, slabs, out = lax.optimization_barrier(
            (near, held, crossed, chunks, late, slabs, out)
        )
        done, after = {}, {}
        i = slot - 1
        if i < count:
            after[i] = near.pop(i)
            if direct < line:
                relay = jnp.where((me_line == 0) | (me_line == 3), after[i][1], after[i][2])
                after[i] = after[i] + [move_line(relay, lambda s: (2, 0, 3, 1)[s])]
        if slot == 1:
            chunks = merge(late)
            late = None
        if slot < count:
            near[slot] = spread(chunks[slot])
        if slot == 1:
            slab_here = lax.dynamic_slice_in_dim(
                jnp.concatenate([first_chunk] + [chunks[c] for c in range(1, count)], axis=1),
                slab_offset[me_tp], SLAB_DEV, 1,
            )
            slabs = [slab_here] + [swap_dp(slab_here, j) for j in range(1, n_dp)]
        if slot == 2:
            slab = joined(slabs)
            slabs = None
        i = slot - 2
        if 0 <= i < count:
            picked = dealt(which, held.pop(i))
            done[i] = [picked[0]] + [swap_dp(picked[j], j) for j in range(1, n_dp)]
        i = slot - 3
        if 0 <= i < count:
            mine = joined(crossed.pop(i))
            other = swap_core(mine)
            if i + 1 < count:
                out = grams(i, (0, 1), mine, other, out)
            else:
                out = grams(i, (0,), mine, other, out)
                out = grams(i, (1,), mine, other, out)
        held.update(after)
        crossed.update(done)
    return out


def mirrored(n_dp, value):
    return lax.ppermute(value, "dp", [(s, n_dp - 1 - s) for s in range(n_dp)])


def share_rows(n_dp, n_tp, room, widths, owns, spares, first, slab_offset, total):
    kept = room - spares[0].shape[0]

    def merged(own, extra):
        return own + jnp.pad(extra, ((kept, 0), (0, 0)))

    def merge(rest):
        starts = [sum(widths[1:i]) for i in range(1, len(widths) + 1)]
        return {c: merged(owns[c], rest[:, starts[c - 1] : starts[c]]) for c in range(1, len(widths))}

    return exchange(
        n_dp, n_tp, widths, merged(owns[0], first), lambda: (mirrored(n_dp, spares[1]), merge), slab_offset, total
    )


def all_rows(n_dp, n_tp, widths, owns, spares, first, slab_offset, total):
    def merge(rest):
        starts = [sum(widths[1:i]) for i in range(1, len(widths) + 1)]
        return {
            c: jnp.concatenate([owns[c], rest[:, starts[c - 1] : starts[c]]], axis=0)
            for c in range(1, len(widths))
        }

    first_chunk = jnp.concatenate([owns[0], spares[0]], axis=0)
    return exchange(n_dp, n_tp, widths, first_chunk, lambda: (spares[1], merge), slab_offset, total)


def on_device(n_dp, n_tp, gate_pre, up_pre, token_live, slab_offset):
    tokens, half = gate_pre.shape
    room = tokens * 11 // 16
    widths = chunk_widths(half)
    live = token_live[None, :]
    masks = [live] + [lax.ppermute(live, "dp", [(s, s ^ j) for s in range(n_dp)]) for j in range(1, n_dp)]
    owns, spares = live_keys(gate_pre, up_pre, live, room, widths)
    first = mirrored(n_dp, spares[0])
    total, fits = tally(masks, room)
    return lax.cond(
        fits[0] > 0,
        functools.partial(share_rows, n_dp, n_tp, room, widths),
        functools.partial(all_rows, n_dp, n_tp, widths),
        owns, spares, first, slab_offset, total,
    )


def solution(mesh):
    placed = (P("dp", "tp"), P("dp", "tp"), P("dp"), P())
    return jax.shard_map(
        functools.partial(on_device, mesh.shape["dp"], mesh.shape["tp"]),
        mesh=mesh,
        in_specs=placed,
        out_specs=P("dp", "tp"),
        check_vma=False,
    )
```

time: 412 us -> 168 us (0.41)
  blocking collectives: 184 us -> 0 us
  waiting for transfers between devices: 137 us -> 56.6 us
  Pallas kernels: 0 us -> 49 us
  starting transfers between devices: 6.82 us -> 42.3 us
  matrix products: 31.8 us -> 0 us
  between operations: 16.7 us -> 0.86 us
  local copies, waits for them, and re-layouts: 29.3 us -> 13.5 us
    psum x1 -> x0, blocking collectives: 184 us -> none  [on_device(): live_total = lax.psum(jnp.sum(live_mask), 'dp')]
    all_gather x2 -> x0, waiting for transfers between devices: 137 us -> none  [the longest x1 137 us: on_device(): all_keys = lax.all_gather(key_local, 'tp', axis=1, tiled=True)]
    ppermute x0 -> x36, waiting for transfers between devices: none -> 56.6 us  [the longest x12 45.8 us: move_line(): lax.ppermute(value, 'tp', [(2 * s + c, 2 * target(s) + c) for s in range(...]
    pallas_call x0 -> x16, Pallas kernels: none -> 49 us  [the longest x5 38.5 us: gram_rows(): pl.pallas_call(gram_kernel, in_specs=in_specs, out_specs=pl.BlockSpec(mem...]
    ppermute x0 -> x36, starting transfers between devices: none -> 42.3 us  [the longest x15 16.6 us: swap_dp(): return lax.ppermute(value, 'dp', [(s, s ^ j) for s in range(n_dp)])]
    dot_general x1 -> x0, matrix products: 31.8 us -> none  [contract_tokens(): lax.dot_general(left, right, (((0,), (0,)), ((), ())), preferred_element_...]
    all_to_all x1 -> x0, local copies, waits for them, and re-layouts: 19.7 us -> none  [on_device(): lax.all_to_all(all_keys, 'dp', split_axis=1, concat_axis=0, tiled=True)]
    all_to_all x1 -> x0, starting transfers between devices: 6.77 us -> none  [on_device(): lax.all_to_all(all_keys, 'dp', split_axis=1, concat_axis=0, tiled=True)]
  transfers between devices with their start and end apart: 3 -> 36, of which waited for: 1 -> 13; matrix products, arithmetic and copies ran while one was open for 6% -> 2% of each run, Pallas kernels for 0% -> 22%
where the time goes in v2:
time: 168 us; the launch traced here: 167 us
  waiting for transfers between devices  56.6 us (34%)
  Pallas kernels  49 us (29%)
  starting transfers between devices  42.3 us (25%)
  local copies, waits for them, and re-layouts  13.5 us (8%)
  other arithmetic  2.42 us (1%)
  loops' own time  2.34 us (1%)
    ppermute x12, waiting for transfers between devices, move_line(): lax.ppermute(value, 'tp', [(2 * s + c, 2 * target(s) + c) for s in range(...  45.8 us
    pallas_call x5, Pallas kernels, gram_rows(): pl.pallas_call(gram_kernel, in_specs=in_specs, out_specs=pl.BlockSpec(mem...  38.5 us
    ppermute x15, starting transfers between devices, swap_dp(): return lax.ppermute(value, 'dp', [(s, s ^ j) for s in range(n_dp)])  16.6 us
    ppermute x12, starting transfers between devices, move_line(): lax.ppermute(value, 'tp', [(2 * s + c, 2 * target(s) + c) for s in range(...  15.3 us
    ppermute x15, waiting for transfers between devices, swap_dp(): return lax.ppermute(value, 'dp', [(s, s ^ j) for s in range(n_dp)])  9.17 us
    ppermute x2, starting transfers between devices, mirrored(): return lax.ppermute(value, 'dp', [(s, n_dp - 1 - s) for s in range(n_dp)])  6.87 us
    cond x52, local copies, waits for them, and re-layouts  6.77 us
    pallas_call x5, Pallas kernels, joined(): pl.pallas_call(join_kernel, in_specs=[pl.BlockSpec(memory_space=pltpu.VME...  5.34 us
  transfers between devices with their start and end apart: 36, of which 13 were waited for; matrix products, arithmetic and copies ran while one was open for 2% of the time, Pallas kernels for 22%

profile of v2, /device:TPU:0, one launch (start us, length us, event | category | flops | bytes accessed | tf_op | source)
XLA Modules:
  0.0 167.1 jit_solution(2209558856133782635)
XLA Ops:
  3.7 3.4 %live_keys.1 = (bf16[176,1024]{1,0:T(8,128)(2,1)S(1)}, bf16[176,1024]{1,0:T(8,128)(2,1)S(1)}, bf16[176,1024]{1,0:T(8,128)(2,1)S(1)}, bf16[176,512]{1,0:T(8,128)(...) custom-call(s32[1,256]{1,0:T(1,128)S(1)} %bitcast.23, bf16[256,3584]{1,0:T(8,128)(2,1)S(1)} %copy-done.18, ...), custom_call_target="tpu_custom_call" | custom-call | flops 469762048 | bytes 5505024 | tf_op jit(solution)/shard_map/live_keys/pallas_call | solution.py:50
  7.0 4.0 %collective-permute-start.66 = (bf16[80,1024]{1,0:T(8,128)(2,1)S(1)}, bf16[80,1024]{1,0:T(8,128)(2,1)S(1)}, u32[]{:S(2)}, u32[]{:S(2)}) collective-permute-start(bf16[80,1024]{1,0:T(8,128)(2,1)S(1)} %get-tuple-element.208), channel_id=1, source_target_pairs={{0,24},{8,16},{16,8},{24,0},{1,25},{9,17},{17,9},{25,1},{2,26},{10... | collective-permute-start | bytes 491528 | tf_op jit(solution)/shard_map/ppermute | solution.py:281
  11.6 2.8 %collective-permute-start.65 = (s32[1,256]{1,0:T(1,128)S(1)}, s32[1,256]{1,0:T(1,128)S(1)}, u32[]{:S(2)}, u32[]{:S(2)}) collective-permute-start(s32[1,256]{1,0:T(1,128)S(1)} %bitcast.26), channel_id=1, source_target_pairs={{0,24},{8,16},{16,8},{24,0},{1,25},{9,17},{17,9},{25,1},{2,26},{10... | collective-permute-start | bytes 3080 | tf_op jit(solution)/shard_map/ppermute | solution.py:316
  18.7 148.2 %conditional.1 = (f32[7168,1536]{1,0:T(8,128)}) conditional(s32[]{:T(128)} %bitcast.21, (bf16[176,1024]{1,0:T(8,128)(2,1)S(1)}, bf16[80,1024]{1,0:T(8,128)(2,1)S(1)}, bf16[80,2560]{1,0:T(8,128)(2,1)S(1)}, bf16[176,1024]{1,0:T(8,128)(2,1)S(1)}, bf16[176,1024]{1,0:T(8,128)(2,1)S(1)}, /*index=5*/bf16[176,512]{1,0:T(8,128)(2,1)S(1)}, s32[8]{0:T(128)S(1)}, ...), branch_computations={%region_0.1_spmd, %region_1.2_spmd} | conditional | flops 22557622272 | bytes 215255744 | solution.py:320
  19.0 2.9 %collective-permute-start.33 = (bf16[80,2560]{1,0:T(8,128)(2,1)S(1)}, bf16[80,2560]{1,0:T(8,128)(2,1)}, u32[]{:S(2)}, u32[]{:S(2)}) collective-permute-start(bf16[80,2560]{1,0:T(8,128)(2,1)S(1)} %get-tuple-element.123), channel_id=1, source_target_pairs={{0,24},{8,16},{16,8},{24,0},{1,25},{9,17},{17,9},{25,1},{2,26},{10... | collective-permute-start | bytes 1228808 | tf_op jit(solution)/shard_map/cond/branch_1_fun/ppermute | solution.py:281
  22.0 1.6 collective-permute-start.31
  23.6 2.6 %collective-permute-start.32 = (bf16[176,1024]{1,0:T(8,128)(2,1)S(1)}, bf16[176,1024]{1,0:T(8,128)(2,1)S(1)}, u32[]{:S(2)}, u32[]{:S(2)}) collective-permute-start(bf16[176,1024]{1,0:T(8,128)(2,1)S(1)} %pad_add_fusion.5.refs_0_), channel_id=1, source_target_pairs={{0,4},{1,5},{2,6},{3,7},{4,0},{5,1},{6,2},{7,3},{8,12},{9,13},{10,... | collective-permute-start | bytes 1081352 | tf_op jit(solution)/shard_map/cond/branch_1_fun/ppermute | solution.py:218
  28.5 9.4 %collective-permute-done.31.refs_1_ = bf16[176,1024]{1,0:T(8,128)(2,1)S(1)} collective-permute-done((bf16[176,1024]{1,0:T(8,128)(2,1)S(1)}, bf16[176,1024]{1,0:T(8,128)(2,1)S(1)}, u32[]{:S(2)}, u32[]{:S(2)}) %collective-permute-start.31) | collective-permute-done | bytes 360480 | tf_op jit(solution)/shard_map/cond/branch_1_fun/ppermute | solution.py:218
  37.9 2.4 %collective-permute-done.32.refs_2_ = bf16[176,1024]{1,0:T(8,128)(2,1)S(1)} collective-permute-done((bf16[176,1024]{1,0:T(8,128)(2,1)S(1)}, bf16[176,1024]{1,0:T(8,128)(2,1)S(1)}, u32[]{:S(2)}, u32[]{:S(2)}) %collective-permute-start.32) | collective-permute-done | bytes 360480 | tf_op jit(solution)/shard_map/cond/branch_1_fun/ppermute | solution.py:218
  46.1 2.1 %collective-permute-start.39 = (bf16[176,1536]{1,0:T(8,128)(2,1)S(1)}, bf16[176,1536]{1,0:T(8,128)(2,1)}, u32[]{:S(2)}, u32[]{:S(2)}) collective-permute-start(bf16[176,1536]{1,0:T(8,128)(2,1)S(1)} %fusion.8.refs_0_), channel_id=1, source_target_pairs={{0,24},{8,16},{16,8},{24,0},{1,25},{9,17},{17,9},{25,1},{2,26},{10... | collective-permute-start | bytes 1622024 | tf_op jit(solution)/shard_map/cond/branch_1_fun/ppermute | solution.py:212
  48.2 1.7 %collective-permute-start.34 = (bf16[176,1024]{1,0:T(8,128)(2,1)S(1)}, bf16[176,1024]{1,0:T(8,128)(2,1)S(1)}, u32[]{:S(2)}, u32[]{:S(2)}) collective-permute-start(bf16[176,1024]{1,0:T(8,128)(2,1)S(1)} %pad_add_fusion.4.refs_0_), channel_id=1, source_target_pairs={{0,2},{1,3},{2,0},{3,1},{4,6},{5,7},{6,4},{7,5},{8,10},{9,11},{10,... | collective-permute-start | bytes 1081352 | tf_op jit(solution)/shard_map/cond/branch_1_fun/ppermute | solution.py:218
  49.9 6.8 %collective-permute-done.36.refs_3_ = bf16[176,1024]{1,0:T(8,128)(2,1)S(1)} collective-permute-done((bf16[176,1024]{1,0:T(8,128)(2,1)S(1)}, bf16[176,1024]{1,0:T(8,128)(2,1)S(1)}, u32[]{:S(2)}, u32[]{:S(2)}) %collective-permute-start.36) | collective-permute-done | bytes 360480 | tf_op jit(solution)/shard_map/cond/branch_1_fun/ppermute | solution.py:218
  57.8 3.5 %collective-permute-done.34.refs_1_ = bf16[176,1024]{1,0:T(8,128)(2,1)S(1)} collective-permute-done((bf16[176,1024]{1,0:T(8,128)(2,1)S(1)}, bf16[176,1024]{1,0:T(8,128)(2,1)S(1)}, u32[]{:S(2)}, u32[]{:S(2)}) %collective-permute-start.34) | collective-permute-done | bytes 360480 | tf_op jit(solution)/shard_map/cond/branch_1_fun/ppermute | solution.py:218
  61.3 8.5 %collective-permute-done.35.refs_2_ = bf16[176,1024]{1,0:T(8,128)(2,1)S(1)} collective-permute-done((bf16[176,1024]{1,0:T(8,128)(2,1)S(1)}, bf16[176,1024]{1,0:T(8,128)(2,1)S(1)}, u32[]{:S(2)}, u32[]{:S(2)}) %collective-permute-start.35) | collective-permute-done | bytes 360480 | tf_op jit(solution)/shard_map/cond/branch_1_fun/ppermute | solution.py:218
  72.5 2.1 %collective-permute-start.45 = (bf16[176,1024]{1,0:T(8,128)(2,1)S(1)}, bf16[176,1024]{1,0:T(8,128)(2,1)S(1)}, u32[]{:S(2)}, u32[]{:S(2)}) collective-permute-start(bf16[176,1024]{1,0:T(8,128)(2,1)S(1)} %get-tuple-element.146), channel_id=1, source_target_pairs={{0,24},{8,16},{16,8},{24,0},{1,25},{9,17},{17,9},{25,1},{2,26},{10... | collective-permute-start | bytes 1081352 | tf_op jit(solution)/shard_map/cond/branch_1_fun/ppermute | solution.py:212
  74.7 2.0 %collective-permute-start.40 = (bf16[176,1024]{1,0:T(8,128)(2,1)S(1)}, bf16[176,1024]{1,0:T(8,128)(2,1)S(1)}, u32[]{:S(2)}, u32[]{:S(2)}) collective-permute-start(bf16[176,1024]{1,0:T(8,128)(2,1)S(1)} %pad_add_fusion.3.refs_0_), channel_id=1, source_target_pairs={{0,2},{1,3},{2,0},{3,1},{4,6},{5,7},{6,4},{7,5},{8,10},{9,11},{10,... | collective-permute-start | bytes 1081352 | tf_op jit(solution)/shard_map/cond/branch_1_fun/ppermute | solution.py:218
  76.7 2.4 %collective-permute-done.43.refs_1_ = bf16[176,1024]{1,0:T(8,128)(2,1)S(1)} collective-permute-done((bf16[176,1024]{1,0:T(8,128)(2,1)S(1)}, bf16[176,1024]{1,0:T(8,128)(2,1)S(1)}, u32[]{:S(2)}, u32[]{:S(2)}) %collective-permute-start.43) | collective-permute-done | bytes 360480 | tf_op jit(solution)/shard_map/cond/branch_1_fun/ppermute | solution.py:212
  79.1 1.9 %collective-permute-start.41 = (bf16[176,1024]{1,0:T(8,128)(2,1)S(1)}, bf16[176,1024]{1,0:T(8,128)(2,1)S(1)}, u32[]{:S(2)}, u32[]{:S(2)}) collective-permute-start(bf16[176,1024]{1,0:T(8,128)(2,1)S(1)} %pad_add_fusion.3.refs_0_), channel_id=1, source_target_pairs={{0,4},{1,5},{2,6},{3,7},{4,0},{5,1},{6,2},{7,3},{8,12},{9,13},{10,... | collective-permute-start | bytes 1081352 | tf_op jit(solution)/shard_map/cond/branch_1_fun/ppermute | solution.py:218
  81.0 2.4 %collective-permute-done.44.refs_2_ = bf16[176,1024]{1,0:T(8,128)(2,1)S(1)} collective-permute-done((bf16[176,1024]{1,0:T(8,128)(2,1)S(1)}, bf16[176,1024]{1,0:T(8,128)(2,1)S(1)}, u32[]{:S(2)}, u32[]{:S(2)}) %collective-permute-start.44) | collective-permute-done | bytes 360480 | tf_op jit(solution)/shard_map/cond/branch_1_fun/ppermute | solution.py:212
  83.4 2.7 %collective-permute-done.42.refs_3_ = bf16[176,1024]{1,0:T(8,128)(2,1)S(1)} collective-permute-done((bf16[176,1024]{1,0:T(8,128)(2,1)S(1)}, bf16[176,1024]{1,0:T(8,128)(2,1)S(1)}, u32[]{:S(2)}, u32[]{:S(2)}) %collective-permute-start.42) | collective-permute-done | bytes 360480 | tf_op jit(solution)/shard_map/cond/branch_1_fun/ppermute | solution.py:218
  86.8 6.7 %collective-permute-done.40.refs_1_ = bf16[176,1024]{1,0:T(8,128)(2,1)S(1)} collective-permute-done((bf16[176,1024]{1,0:T(8,128)(2,1)S(1)}, bf16[176,1024]{1,0:T(8,128)(2,1)S(1)}, u32[]{:S(2)}, u32[]{:S(2)}) %collective-permute-start.40) | collective-permute-done | bytes 360480 | tf_op jit(solution)/shard_map/cond/branch_1_fun/ppermute | solution.py:218
  96.3 1.6 joined.15.refs_0_
  98.6 2.4 %collective-permute-start.47 = (bf16[176,512]{1,0:T(8,128)(2,1)S(1)}, bf16[176,512]{1,0:T(8,128)(2,1)S(1)}, u32[]{:S(2)}, u32[]{:S(2)}) collective-permute-start(bf16[176,512]{1,0:T(8,128)(2,1)S(1)} %copy-done.21), channel_id=1, source_target_pairs={{0,4},{1,5},{2,6},{3,7},{4,0},{5,1},{6,2},{7,3},{8,12},{9,13},{10,... | collective-permute-start | bytes 540680 | tf_op jit(solution)/shard_map/cond/branch_1_fun/ppermute | solution.py:218
  102.6 5.9 %collective-permute-done.46.refs_1_ = bf16[176,512]{1,0:T(8,128)(2,1)S(1)} collective-permute-done((bf16[176,512]{1,0:T(8,128)(2,1)S(1)}, bf16[176,512]{1,0:T(8,128)(2,1)S(1)}, u32[]{:S(2)}, u32[]{:S(2)}) %collective-permute-start.46) | collective-permute-done | bytes 180256 | tf_op jit(solution)/shard_map/cond/branch_1_fun/ppermute | solution.py:218
  109.5 10.2 %gram_rows.15.refs_3_ = f32[7168,1536]{1,0:T(8,128)} custom-call(s32[2]{0:T(128)S(1)} %pad_add_fusion.7.rows_ref, f32[1]{0:T(128)} %get-tuple-element.119.total_ref, bf16[704,1536]{1,0:T(8,128)(2,1)S(1)} %joined.15.refs_0_, bf16[704,1024]{1,0:T(8,128)(2,1)} %joined.16.refs_1_, bf16[704,1024]{1,0:T(8,128)(2,1)} %collective-permute-done.52.refs_2_), custom_call_target="tpu_custom_call" | custom-call | flops 4429185024 | bytes 12582912 | tf_op jit(solution)/shard_map/cond/branch_1_fun/gram_rows/pallas_call | solution.py:154
  126.5 1.5 collective-permute-start.53
  128.0 10.2 %gram_rows.16.refs_3_ = f32[7168,1536]{1,0:T(8,128)} custom-call(s32[2]{0:T(128)S(1)} %pad_add_fusion.8.rows_ref, f32[1]{0:T(128)} %get-tuple-element.119.total_ref, bf16[704,1536]{1,0:T(8,128)(2,1)S(1)} %joined.15.refs_0_, bf16[704,1024]{1,0:T(8,128)(2,1)} %joined.17.refs_1_, ...), custom_call_target="tpu_custom_call", output_to_operand_aliasing={{}: (5, {})} | custom-call | flops 4429185024 | bytes 12582912 | tf_op jit(solution)/shard_map/cond/branch_1_fun/gram_rows/pallas_call | solution.py:154
  138.3 4.4 %collective-permute-done.55.refs_2_ = bf16[176,1024]{1,0:T(8,128)(2,1)S(1)} collective-permute-done((bf16[176,1024]{1,0:T(8,128)(2,1)S(1)}, bf16[176,1024]{1,0:T(8,128)(2,1)S(1)}, u32[]{:S(2)}, u32[]{:S(2)}) %collective-permute-start.55) | collective-permute-done | bytes 360480 | tf_op jit(solution)/shard_map/cond/branch_1_fun/ppermute | solution.py:212
  146.8 1.8 %collective-permute-start.60 = (bf16[176,512]{1,0:T(8,128)(2,1)S(1)}, bf16[176,512]{1,0:T(8,128)(2,1)S(1)}, u32[]{:S(2)}, u32[]{:S(2)}) collective-permute-start(bf16[176,512]{1,0:T(8,128)(2,1)S(1)} %get-tuple-element.187), channel_id=1, source_target_pairs={{0,24},{8,16},{16,8},{24,0},{1,25},{9,17},{17,9},{25,1},{2,26},{10... | collective-permute-start | bytes 540680 | tf_op jit(solution)/shard_map/cond/branch_1_fun/ppermute | solution.py:212
  148.5 10.2 %gram_rows.17.refs_2_ = f32[7168,1536]{1,0:T(8,128)} custom-call(s32[2]{0:T(128)S(1)} %pad_add_fusion.9.rows_ref, f32[1]{0:T(128)} %get-tuple-element.119.total_ref, bf16[704,1536]{1,0:T(8,128)(2,1)S(1)} %joined.15.refs_0_, bf16[704,1024]{1,0:T(8,128)(2,1)} %joined.18.refs_1_, ...), custom_call_target="tpu_custom_call", output_to_operand_aliasing={{}: (5, {})} | custom-call | flops 4429185024 | bytes 12582912 | tf_op jit(solution)/shard_map/cond/branch_1_fun/gram_rows/pallas_call | solution.py:154
  158.9 3.5 %gram_rows.18.refs_2_ = f32[7168,1536]{1,0:T(8,128)} custom-call(s32[1]{0:T(128)} %bitcast.19.rows_ref, f32[1]{0:T(128)} %get-tuple-element.119.total_ref, bf16[704,1536]{1,0:T(8,128)(2,1)S(1)} %joined.15.refs_0_, bf16[704,512]{1,0:T(8,128)(2,1)S(1)} %joined.19.refs_1_, f32[7168,1536]{1,0:T(8,128)} %gram_rows.17.refs_2_), custom_call_target="tpu_custom_call", output_to_operand_aliasing={{}: (4, {})} | custom-call | flops 1107296256 | bytes 3145728 | tf_op jit(solution)/shard_map/cond/branch_1_fun/gram_rows/pallas_call | solution.py:154
  162.4 4.6 %gram_rows.19 = f32[7168,1536]{1,0:T(8,128)} custom-call(s32[1]{0:T(128)} %bitcast.10.rows_ref, f32[1]{0:T(128)} %get-tuple-element.119.total_ref, bf16[704,1536]{1,0:T(8,128)(2,1)S(1)} %joined.15.refs_0_, bf16[704,512]{1,0:T(8,128)(2,1)} %collective-permute-done.62.refs_1_, f32[7168,1536]{1,0:T(8,128)} %gram_rows.18.refs_2_), custom_call_target="tpu_custom_call", output_to_operand_aliasing={{}: (4, {})} | custom-call | flops 1107296256 | bytes 3145728 | tf_op jit(solution)/shard_map/cond/branch_1_fun/gram_rows/pallas_call | solution.py:154
  (138 shorter events, 36.0 us)
Async XLA Ops:
  7.0 11.7 %collective-permute-start.66 = (bf16[80,1024]{1,0:T(8,128)(2,1)S(1)}, bf16[80,1024]{1,0:T(8,128)(2,1)S(1)}, u32[]{:S(2)}, u32[]{:S(2)}) collective-permute-start(bf16[80,1024]{1,0:T(8,128)(2,1)S(1)} %get-tuple-element.208), channel_id=1, source_target_pairs={{0,24},{8,16},{16,8},{24,0},{1,25},{9,17},{17,9},{25,1},{2,26},{10... | collective-permute-start | bytes 491528 | tf_op jit(solution)/shard_map/ppermute | solution.py:281
  19.0 21.3 %collective-permute-start.33 = (bf16[80,2560]{1,0:T(8,128)(2,1)S(1)}, bf16[80,2560]{1,0:T(8,128)(2,1)}, u32[]{:S(2)}, u32[]{:S(2)}) collective-permute-start(bf16[80,2560]{1,0:T(8,128)(2,1)S(1)} %get-tuple-element.123), channel_id=1, source_target_pairs={{0,24},{8,16},{16,8},{24,0},{1,25},{9,17},{17,9},{25,1},{2,26},{10... | collective-permute-start | bytes 1228808 | tf_op jit(solution)/shard_map/cond/branch_1_fun/ppermute | solution.py:281
  22.0 15.9 %collective-permute-start.31 = (bf16[176,1024]{1,0:T(8,128)(2,1)S(1)}, bf16[176,1024]{1,0:T(8,128)(2,1)S(1)}, u32[]{:S(2)}, u32[]{:S(2)}) collective-permute-start(bf16[176,1024]{1,0:T(8,128)(2,1)S(1)} %pad_add_fusion.5.refs_0_), channel_id=1, source_target_pairs={{0,2},{1,3},{2,0},{3,1},{4,6},{5,7},{6,4},{7,5},{8,10},{9,11},{10,... | collective-permute-start | bytes 1081352 | tf_op jit(solution)/shard_map/cond/branch_1_fun/ppermute | solution.py:218
  23.6 16.6 %collective-permute-start.32 = (bf16[176,1024]{1,0:T(8,128)(2,1)S(1)}, bf16[176,1024]{1,0:T(8,128)(2,1)S(1)}, u32[]{:S(2)}, u32[]{:S(2)}) collective-permute-start(bf16[176,1024]{1,0:T(8,128)(2,1)S(1)} %pad_add_fusion.5.refs_0_), channel_id=1, source_target_pairs={{0,4},{1,5},{2,6},{3,7},{4,0},{5,1},{6,2},{7,3},{8,12},{9,13},{10,... | collective-permute-start | bytes 1081352 | tf_op jit(solution)/shard_map/cond/branch_1_fun/ppermute | solution.py:218
  42.2 14.4 %collective-permute-start.36 = (bf16[176,1024]{1,0:T(8,128)(2,1)S(1)}, bf16[176,1024]{1,0:T(8,128)(2,1)S(1)}, u32[]{:S(2)}, u32[]{:S(2)}) collective-permute-start(bf16[176,1024]{1,0:T(8,128)(2,1)S(1)} %broadcast_select_fusion.6), channel_id=1, source_target_pairs={{0,4},{1,5},{2,0},{3,1},{4,6},{5,7},{6,2},{7,3},{8,12},{9,13},{10,... | collective-permute-start | bytes 1081352 | tf_op jit(solution)/shard_map/cond/branch_1_fun/ppermute | solution.py:218
  44.7 25.2 %collective-permute-start.37 = (bf16[176,1536]{1,0:T(8,128)(2,1)S(1)}, bf16[176,1536]{1,0:T(8,128)(2,1)}, u32[]{:S(2)}, u32[]{:S(2)}) collective-permute-start(bf16[176,1536]{1,0:T(8,128)(2,1)S(1)} %fusion.8.refs_0_), channel_id=1, source_target_pairs={{0,8},{8,0},{16,24},{24,16},{1,9},{9,1},{17,25},{25,17},{2,10},{10... | collective-permute-start | bytes 1622024 | tf_op jit(solution)/shard_map/cond/branch_1_fun/ppermute | solution.py:212
  45.3 24.5 %collective-permute-start.38 = (bf16[176,1536]{1,0:T(8,128)(2,1)S(1)}, bf16[176,1536]{1,0:T(8,128)(2,1)}, u32[]{:S(2)}, u32[]{:S(2)}) collective-permute-start(bf16[176,1536]{1,0:T(8,128)(2,1)S(1)} %fusion.8.refs_0_), channel_id=1, source_target_pairs={{0,16},{8,24},{16,0},{24,8},{1,17},{9,25},{17,1},{25,9},{2,18},{10... | collective-permute-start | bytes 1622024 | tf_op jit(solution)/shard_map/cond/branch_1_fun/ppermute | solution.py:212
  46.1 23.7 %collective-permute-start.39 = (bf16[176,1536]{1,0:T(8,128)(2,1)S(1)}, bf16[176,1536]{1,0:T(8,128)(2,1)}, u32[]{:S(2)}, u32[]{:S(2)}) collective-permute-start(bf16[176,1536]{1,0:T(8,128)(2,1)S(1)} %fusion.8.refs_0_), channel_id=1, source_target_pairs={{0,24},{8,16},{16,8},{24,0},{1,25},{9,17},{17,9},{25,1},{2,26},{10... | collective-permute-start | bytes 1622024 | tf_op jit(solution)/shard_map/cond/branch_1_fun/ppermute | solution.py:212
  48.2 13.1 %collective-permute-start.34 = (bf16[176,1024]{1,0:T(8,128)(2,1)S(1)}, bf16[176,1024]{1,0:T(8,128)(2,1)S(1)}, u32[]{:S(2)}, u32[]{:S(2)}) collective-permute-start(bf16[176,1024]{1,0:T(8,128)(2,1)S(1)} %pad_add_fusion.4.refs_0_), channel_id=1, source_target_pairs={{0,2},{1,3},{2,0},{3,1},{4,6},{5,7},{6,4},{7,5},{8,10},{9,11},{10,... | collective-permute-start | bytes 1081352 | tf_op jit(solution)/shard_map/cond/branch_1_fun/ppermute | solution.py:218
  57.4 12.4 %collective-permute-start.35 = (bf16[176,1024]{1,0:T(8,128)(2,1)S(1)}, bf16[176,1024]{1,0:T(8,128)(2,1)S(1)}, u32[]{:S(2)}, u32[]{:S(2)}) collective-permute-start(bf16[176,1024]{1,0:T(8,128)(2,1)S(1)} %pad_add_fusion.4.refs_0_), channel_id=1, source_target_pairs={{0,4},{1,5},{2,6},{3,7},{4,0},{5,1},{6,2},{7,3},{8,12},{9,13},{10,... | collective-permute-start | bytes 1081352 | tf_op jit(solution)/shard_map/cond/branch_1_fun/ppermute | solution.py:218
  71.1 8.1 %collective-permute-start.43 = (bf16[176,1024]{1,0:T(8,128)(2,1)S(1)}, bf16[176,1024]{1,0:T(8,128)(2,1)S(1)}, u32[]{:S(2)}, u32[]{:S(2)}) collective-permute-start(bf16[176,1024]{1,0:T(8,128)(2,1)S(1)} %get-tuple-element.144), channel_id=1, source_target_pairs={{0,8},{8,0},{16,24},{24,16},{1,9},{9,1},{17,25},{25,17},{2,10},{10... | collective-permute-start | bytes 1081352 | tf_op jit(solution)/shard_map/cond/branch_1_fun/ppermute | solution.py:212
  71.7 11.7 %collective-permute-start.44 = (bf16[176,1024]{1,0:T(8,128)(2,1)S(1)}, bf16[176,1024]{1,0:T(8,128)(2,1)S(1)}, u32[]{:S(2)}, u32[]{:S(2)}) collective-permute-start(bf16[176,1024]{1,0:T(8,128)(2,1)S(1)} %get-tuple-element.145), channel_id=1, source_target_pairs={{0,16},{8,24},{16,0},{24,8},{1,17},{9,25},{17,1},{25,9},{2,18},{10... | collective-permute-start | bytes 1081352 | tf_op jit(solution)/shard_map/cond/branch_1_fun/ppermute | solution.py:212
  72.5 10.8 %collective-permute-start.45 = (bf16[176,1024]{1,0:T(8,128)(2,1)S(1)}, bf16[176,1024]{1,0:T(8,128)(2,1)S(1)}, u32[]{:S(2)}, u32[]{:S(2)}) collective-permute-start(bf16[176,1024]{1,0:T(8,128)(2,1)S(1)} %get-tuple-element.146), channel_id=1, source_target_pairs={{0,24},{8,16},{16,8},{24,0},{1,25},{9,17},{17,9},{25,1},{2,26},{10... | collective-permute-start | bytes 1081352 | tf_op jit(solution)/shard_map/cond/branch_1_fun/ppermute | solution.py:212
  74.7 11.4 %collective-permute-start.42 = (bf16[176,1024]{1,0:T(8,128)(2,1)S(1)}, bf16[176,1024]{1,0:T(8,128)(2,1)S(1)}, u32[]{:S(2)}, u32[]{:S(2)}) collective-permute-start(bf16[176,1024]{1,0:T(8,128)(2,1)S(1)} %broadcast_select_fusion.5), channel_id=1, source_target_pairs={{0,4},{1,5},{2,0},{3,1},{4,6},{5,7},{6,2},{7,3},{8,12},{9,13},{10,... | collective-permute-start | bytes 1081352 | tf_op jit(solution)/shard_map/cond/branch_1_fun/ppermute | solution.py:218
  74.7 18.7 %collective-permute-start.40 = (bf16[176,1024]{1,0:T(8,128)(2,1)S(1)}, bf16[176,1024]{1,0:T(8,128)(2,1)S(1)}, u32[]{:S(2)}, u32[]{:S(2)}) collective-permute-start(bf16[176,1024]{1,0:T(8,128)(2,1)S(1)} %pad_add_fusion.3.refs_0_), channel_id=1, source_target_pairs={{0,2},{1,3},{2,0},{3,1},{4,6},{5,7},{6,4},{7,5},{8,10},{9,11},{10,... | collective-permute-start | bytes 1081352 | tf_op jit(solution)/shard_map/cond/branch_1_fun/ppermute | solution.py:218
  79.1 14.3 %collective-permute-start.41 = (bf16[176,1024]{1,0:T(8,128)(2,1)S(1)}, bf16[176,1024]{1,0:T(8,128)(2,1)S(1)}, u32[]{:S(2)}, u32[]{:S(2)}) collective-permute-start(bf16[176,1024]{1,0:T(8,128)(2,1)S(1)} %pad_add_fusion.3.refs_0_), channel_id=1, source_target_pairs={{0,4},{1,5},{2,6},{3,7},{4,0},{5,1},{6,2},{7,3},{8,12},{9,13},{10,... | collective-permute-start | bytes 1081352 | tf_op jit(solution)/shard_map/cond/branch_1_fun/ppermute | solution.py:218
  96.2 13.4 %collective-permute-start.52 = (bf16[704,1024]{1,0:T(8,128)(2,1)}, bf16[704,1024]{1,0:T(8,128)(2,1)}, u32[]{:S(2)}, u32[]{:S(2)}) collective-permute-start(bf16[704,1024]{1,0:T(8,128)(2,1)} %joined.16.refs_1_), channel_id=1, source_target_pairs={{0,1},{1,0},{2,3},{3,2},{4,5},{5,4},{6,7},{7,6},{8,9},{9,8},{10,11... | collective-permute-start | bytes 4325384 | tf_op jit(solution)/shard_map/cond/branch_1_fun/ppermute | solution.py:215
  97.9 10.7 %collective-permute-start.46 = (bf16[176,512]{1,0:T(8,128)(2,1)S(1)}, bf16[176,512]{1,0:T(8,128)(2,1)S(1)}, u32[]{:S(2)}, u32[]{:S(2)}) collective-permute-start(bf16[176,512]{1,0:T(8,128)(2,1)S(1)} %copy-done.21), channel_id=1, source_target_pairs={{0,2},{1,3},{2,0},{3,1},{4,6},{5,7},{6,4},{7,5},{8,10},{9,11},{10,... | collective-permute-start | bytes 540680 | tf_op jit(solution)/shard_map/cond/branch_1_fun/ppermute | solution.py:218
  98.6 21.1 %collective-permute-start.47 = (bf16[176,512]{1,0:T(8,128)(2,1)S(1)}, bf16[176,512]{1,0:T(8,128)(2,1)S(1)}, u32[]{:S(2)}, u32[]{:S(2)}) collective-permute-start(bf16[176,512]{1,0:T(8,128)(2,1)S(1)} %copy-done.21), channel_id=1, source_target_pairs={{0,4},{1,5},{2,6},{3,7},{4,0},{5,1},{6,2},{7,3},{8,12},{9,13},{10,... | collective-permute-start | bytes 540680 | tf_op jit(solution)/shard_map/cond/branch_1_fun/ppermute | solution.py:218
  101.1 19.3 %collective-permute-start.49 = (bf16[176,1024]{1,0:T(8,128)(2,1)S(1)}, bf16[176,1024]{1,0:T(8,128)(2,1)S(1)}, u32[]{:S(2)}, u32[]{:S(2)}) collective-permute-start(bf16[176,1024]{1,0:T(8,128)(2,1)S(1)} %get-tuple-element.157), channel_id=1, source_target_pairs={{0,8},{8,0},{16,24},{24,16},{1,9},{9,1},{17,25},{25,17},{2,10},{10... | collective-permute-start | bytes 1081352 | tf_op jit(solution)/shard_map/cond/branch_1_fun/ppermute | solution.py:212
  101.9 18.5 %collective-permute-start.50 = (bf16[176,1024]{1,0:T(8,128)(2,1)S(1)}, bf16[176,1024]{1,0:T(8,128)(2,1)S(1)}, u32[]{:S(2)}, u32[]{:S(2)}) collective-permute-start(bf16[176,1024]{1,0:T(8,128)(2,1)S(1)} %get-tuple-element.158), channel_id=1, source_target_pairs={{0,16},{8,24},{16,0},{24,8},{1,17},{9,25},{17,1},{25,9},{2,18},{10... | collective-permute-start | bytes 1081352 | tf_op jit(solution)/shard_map/cond/branch_1_fun/ppermute | solution.py:212
  108.6 11.9 %collective-permute-start.51 = (bf16[176,1024]{1,0:T(8,128)(2,1)S(1)}, bf16[176,1024]{1,0:T(8,128)(2,1)S(1)}, u32[]{:S(2)}, u32[]{:S(2)}) collective-permute-start(bf16[176,1024]{1,0:T(8,128)(2,1)S(1)} %get-tuple-element.159), channel_id=1, source_target_pairs={{0,24},{8,16},{16,8},{24,0},{1,25},{9,17},{17,9},{25,1},{2,26},{10... | collective-permute-start | bytes 1081352 | tf_op jit(solution)/shard_map/cond/branch_1_fun/ppermute | solution.py:212
  109.5 10.9 %collective-permute-start.48 = (bf16[176,1024]{1,0:T(8,128)(2,1)S(1)}, bf16[176,1024]{1,0:T(8,128)(2,1)S(1)}, u32[]{:S(2)}, u32[]{:S(2)}) collective-permute-start(bf16[176,1024]{1,0:T(8,128)(2,1)S(1)} %broadcast_select_fusion.4), channel_id=1, source_target_pairs={{0,4},{1,5},{2,0},{3,1},{4,6},{5,7},{6,2},{7,3},{8,12},{9,13},{10,... | collective-permute-start | bytes 1081352 | tf_op jit(solution)/shard_map/cond/branch_1_fun/ppermute | solution.py:218
  121.7 6.3 %collective-permute-start.57 = (bf16[704,1024]{1,0:T(8,128)(2,1)}, bf16[704,1024]{1,0:T(8,128)(2,1)}, u32[]{:S(2)}, u32[]{:S(2)}) collective-permute-start(bf16[704,1024]{1,0:T(8,128)(2,1)} %joined.17.refs_1_), channel_id=1, source_target_pairs={{0,1},{1,0},{2,3},{3,2},{4,5},{5,4},{6,7},{7,6},{8,9},{9,8},{10,11... | collective-permute-start | bytes 4325384 | tf_op jit(solution)/shard_map/cond/branch_1_fun/ppermute | solution.py:215
  122.9 15.3 %collective-permute-start.54 = (bf16[176,1024]{1,0:T(8,128)(2,1)S(1)}, bf16[176,1024]{1,0:T(8,128)(2,1)S(1)}, u32[]{:S(2)}, u32[]{:S(2)}) collective-permute-start(bf16[176,1024]{1,0:T(8,128)(2,1)S(1)} %get-tuple-element.172), channel_id=1, source_target_pairs={{0,8},{8,0},{16,24},{24,16},{1,9},{9,1},{17,25},{25,17},{2,10},{10... | collective-permute-start | bytes 1081352 | tf_op jit(solution)/shard_map/cond/branch_1_fun/ppermute | solution.py:212
  124.4 18.3 %collective-permute-start.55 = (bf16[176,1024]{1,0:T(8,128)(2,1)S(1)}, bf16[176,1024]{1,0:T(8,128)(2,1)S(1)}, u32[]{:S(2)}, u32[]{:S(2)}) collective-permute-start(bf16[176,1024]{1,0:T(8,128)(2,1)S(1)} %get-tuple-element.173), channel_id=1, source_target_pairs={{0,16},{8,24},{16,0},{24,8},{1,17},{9,25},{17,1},{25,9},{2,18},{10... | collective-permute-start | bytes 1081352 | tf_op jit(solution)/shard_map/cond/branch_1_fun/ppermute | solution.py:212
  125.5 17.2 %collective-permute-start.56 = (bf16[176,1024]{1,0:T(8,128)(2,1)S(1)}, bf16[176,1024]{1,0:T(8,128)(2,1)S(1)}, u32[]{:S(2)}, u32[]{:S(2)}) collective-permute-start(bf16[176,1024]{1,0:T(8,128)(2,1)S(1)} %get-tuple-element.174), channel_id=1, source_target_pairs={{0,24},{8,16},{16,8},{24,0},{1,25},{9,17},{17,9},{25,1},{2,26},{10... | collective-permute-start | bytes 1081352 | tf_op jit(solution)/shard_map/cond/branch_1_fun/ppermute | solution.py:212
  126.5 11.7 %collective-permute-start.53 = (bf16[176,512]{1,0:T(8,128)(2,1)S(1)}, bf16[176,512]{1,0:T(8,128)(2,1)S(1)}, u32[]{:S(2)}, u32[]{:S(2)}) collective-permute-start(bf16[176,512]{1,0:T(8,128)(2,1)S(1)} %broadcast_select_fusion.7), channel_id=1, source_target_pairs={{0,4},{1,5},{2,0},{3,1},{4,6},{5,7},{6,2},{7,3},{8,12},{9,13},{10,... | collective-permute-start | bytes 540680 | tf_op jit(solution)/shard_map/cond/branch_1_fun/ppermute | solution.py:218
  143.9 4.6 %collective-permute-start.61 = (bf16[704,1024]{1,0:T(8,128)(2,1)}, bf16[704,1024]{1,0:T(8,128)(2,1)}, u32[]{:S(2)}, u32[]{:S(2)}) collective-permute-start(bf16[704,1024]{1,0:T(8,128)(2,1)} %joined.18.refs_1_), channel_id=1, source_target_pairs={{0,1},{1,0},{2,3},{3,2},{4,5},{5,4},{6,7},{7,6},{8,9},{9,8},{10,11... | collective-permute-start | bytes 4325384 | tf_op jit(solution)/shard_map/cond/branch_1_fun/ppermute | solution.py:215
  145.0 13.7 %collective-permute-start.58 = (bf16[176,512]{1,0:T(8,128)(2,1)S(1)}, bf16[176,512]{1,0:T(8,128)(2,1)S(1)}, u32[]{:S(2)}, u32[]{:S(2)}) collective-permute-start(bf16[176,512]{1,0:T(8,128)(2,1)S(1)} %get-tuple-element.185), channel_id=1, source_target_pairs={{0,8},{8,0},{16,24},{24,16},{1,9},{9,1},{17,25},{25,17},{2,10},{10... | collective-permute-start | bytes 540680 | tf_op jit(solution)/shard_map/cond/branch_1_fun/ppermute | solution.py:212
  145.8 12.9 %collective-permute-start.59 = (bf16[176,512]{1,0:T(8,128)(2,1)S(1)}, bf16[176,512]{1,0:T(8,128)(2,1)S(1)}, u32[]{:S(2)}, u32[]{:S(2)}) collective-permute-start(bf16[176,512]{1,0:T(8,128)(2,1)S(1)} %get-tuple-element.186), channel_id=1, source_target_pairs={{0,16},{8,24},{16,0},{24,8},{1,17},{9,25},{17,1},{25,9},{2,18},{10... | collective-permute-start | bytes 540680 | tf_op jit(solution)/shard_map/cond/branch_1_fun/ppermute | solution.py:212
  146.8 12.0 %collective-permute-start.60 = (bf16[176,512]{1,0:T(8,128)(2,1)S(1)}, bf16[176,512]{1,0:T(8,128)(2,1)S(1)}, u32[]{:S(2)}, u32[]{:S(2)}) collective-permute-start(bf16[176,512]{1,0:T(8,128)(2,1)S(1)} %get-tuple-element.187), channel_id=1, source_target_pairs={{0,24},{8,16},{16,8},{24,0},{1,25},{9,17},{17,9},{25,1},{2,26},{10... | collective-permute-start | bytes 540680 | tf_op jit(solution)/shard_map/cond/branch_1_fun/ppermute | solution.py:212
  (37 other events, 229.0 us)
